TPU v7x, 128 devices: a whole 4x4x4 slice. The times are simulated.
128 devices in a mesh: row: 2 (over core), col: 64 (over z, y, x).
Axes of the slice: x: 4, y: 4, z: 4, core: 2. Of those that a mesh axis runs over, the one named last changes fastest.
Arguments:
- features: bfloat16 [512, 8192], P('col', 'row'), may hold values from -6 to 6
- a_blocks: bfloat16 [64, 2, 2, 128, 128], P('row'), may hold values from -0.375 to 0.375
- block_cols: int32 [64, 2, 2], P('row'), may hold values from 0 to 31
- block_counts: int32 [64, 2], P('row'), may hold values from 0 to 2
- weight: bfloat16 [512, 512], P('col'), may hold values from -0.25 to 0.25
- cotangent: bfloat16 [512, 8192], P('col', 'row'), may hold values from -6 to 6
Outputs:
- output: bfloat16 [512, 8192], P('col', 'row')
- grad_weight: float32 [512, 512], P('col')
- grad_features: bfloat16 [512, 8192], P('col', 'row')
Inputs may be any that keep to these rules, and one draw needn't show every extreme that they name: `block_cols`: block column indices lie within one slab's blocks.
All inputs are finite; a program needn't handle non-finite values.
Results may differ from a plain program's by a relative error of at most 0.0061.
Values may be sent and summed in bfloat16 or wider, within the bound.
No kernel may reach another device: no remote copies, remote signals or barrier semaphores. Data moves between devices by JAX's collectives and lax.ppermute only.
A program may use at most 128 MiB of HBM per device.

v0:
```python
import jax
import jax.numpy as jnp
from jax import lax
from jax.sharding import PartitionSpec as P


def from_root(value, axis, source):
    kept = jnp.where(lax.axis_index(axis) == source, value, 0).astype(value.dtype)
    return lax.psum(kept, axis)


def local(features, a_blocks, block_cols, block_counts, weight, cotangent):
    feat_dev = features.shape[0]
    slab_rows = features.shape[1]
    block_size = a_blocks.shape[-1]
    local_blocks = a_blocks.shape[0]
    section_count = a_blocks.shape[1]
    slot_count = a_blocks.shape[2]
    row_blocks = slab_rows // block_size
    slot_ids = jnp.arange(slot_count, dtype=jnp.int32)
    live_mask = (slot_ids[None, None, :] < block_counts[:, :, None]).astype(jnp.bfloat16)
    masked = a_blocks * live_mask[:, :, :, None, None]
    global_index = (
        jnp.arange(section_count, dtype=jnp.int32)[None, :, None] * row_blocks + block_cols
    )
    node_total = slab_rows * lax.axis_size("row")
    total = jnp.zeros((feat_dev, local_blocks, block_size), jnp.float32)
    for section_idx in range(lax.axis_size("row")):
        panel_rows = from_root(features, "row", section_idx).reshape(
            feat_dev, row_blocks, block_size
        )
        picked = panel_rows[:, block_cols[:, section_idx, :]]
        total = total + jnp.einsum(
            "fbkj,bkij->fbi", picked, masked[:, section_idx], preferred_element_type=jnp.float32
        )
    aggregated = total.reshape(feat_dev, slab_rows).astype(jnp.bfloat16)
    agg_full = lax.all_gather(aggregated, "col", axis=0, tiled=True)
    preact = jnp.dot(weight, agg_full, preferred_element_type=jnp.float32)
    output = jax.nn.silu(preact).astype(jnp.bfloat16)
    sigmoid_pre = jax.nn.sigmoid(preact)
    dpre = (
        cotangent.astype(jnp.float32) * sigmoid_pre * (1.0 + preact * (1.0 - sigmoid_pre))
    ).astype(jnp.bfloat16)
    local_grad = lax.dot_general(
        dpre, agg_full, (((1,), (1,)), ((), ())), preferred_element_type=jnp.float32
    )
    grad_weight = lax.psum(local_grad, "row") / jnp.sqrt(jnp.float32(node_total))
    dagg = lax.psum_scatter(
        lax.dot_general(weight, dpre, (((0,), (0,)), ((), ())), preferred_element_type=jnp.float32),
        "col",
        scatter_dimension=0,
        tiled=True,
    ).astype(jnp.bfloat16)
    contrib = jnp.einsum(
        "fbi,bskij->fbskj",
        dagg.reshape(feat_dev, local_blocks, block_size),
        masked,
        preferred_element_type=jnp.float32,
    )
    terms = (
        jnp.zeros((feat_dev, section_count * row_blocks, block_size), jnp.float32)
        .at[:, global_index]
        .add(contrib)
    )
    terms = terms.reshape(feat_dev, section_count * slab_rows)
    grad_features = lax.psum_scatter(terms, "row", scatter_dimension=1, tiled=True).astype(
        jnp.bfloat16
    )
    return (output, grad_weight, grad_features)


def solution(mesh):
    placed = (
        P("col", "row"),
        P("row", None, None, None, None),
        P("row", None, None),
        P("row", None),
        P("col", None),
        P("col", "row"),
    )
    return jax.shard_map(
        local,
        mesh=mesh,
        in_specs=placed,
        out_specs=(P("col", "row"), P("col", None), P("col", "row")),
        check_vma=False,
    )
```

profile of v0, /device:TPU:1, one launch (start us, length us, event | category | flops | bytes accessed | tf_op | source)
XLA Modules:
  0.0 526.8 jit_solution(13644027681223521982)
XLA Ops:
  7.2 1.5 select_bitcast_fusion
  8.8 0.0 all-gather.2.cloned.1.call-start
  8.8 0.7 compare_select_fusion.1
  9.5 0.1 copy.22
  9.6 0.1 reshape.92
  9.7 0.8 fusion.9
  10.5 4.5 copy_multiply_fusion
  15.0 0.1 copy.23
  15.1 0.1 reshape.100
  15.2 23.0 %all-reduce.3.cloned.1.call-done = (bf16[8,32,128]{2,0,1:T(8,128)(2,1)}, bf16[8,32,128]{2,0,1:T(8,128)(2,1)}) async-done(((bf16[8,32,128]{2,0,1:T(8,128)(2,1)}, bf16[8,32,128]{2,0,1:T(8,128)(2,1)}), (bf16[8,32,128]{2,0,1:T(8,128)(2,1)}, bf16[8,32,128]{2,0,1:T(8,128)(2,1)})) %all-reduce.3.cloned.1.call-update) | async-done | bytes 131088 | tf_op jit(solution)/shard_map/psum | solution.py:9
  38.2 1.5 gather_fusion
  39.7 2.2 fusion.4
  41.9 1.5 gather_fusion.1
  43.4 2.9 fusion.8
  46.4 0.0 reduce-scatter.7.cloned.1.call-start
  46.4 68.5 %all-gather.2.cloned.1.call-done = bf16[512,4096]{1,0:T(8,128)(2,1)} async-done(((bf16[8,4096]{1,0:T(8,128)(2,1)}), bf16[512,4096]{1,0:T(8,128)(2,1)}) %all-gather.2.cloned.1.call-update) | async-done | bytes 4194320 | tf_op jit(solution)/shard_map/all_gather | solution.py:37
  114.9 3.5 multiply_convert_fusion.1
  118.3 4.5 convolution_bitcast_fusion
  122.9 8.9 %copy.32 = f32[512,4096]{1,0:T(8,128)} copy(f32[512,4096]{0,1:T(8,128)} %convolution_bitcast_fusion) | data formatting | bytes 16777216
  131.9 0.6 copy-done.3
  132.5 0.1 compare_select_fusion
  132.6 0.1 copy.24
  132.7 0.1 reshape.108
  132.8 323.2 %reduce-scatter.7.cloned.1.call-done = f32[8,4096]{1,0:T(8,128)} async-done(((f32[512,4096]{1,0:T(8,128)}), f32[8,4096]{1,0:T(8,128)}) %reduce-scatter.7.cloned.1.call-update) | async-done | bytes 131088
  456.0 1.4 copy.33
  457.4 2.9 fusion
  460.4 4.9 scatter_fusion
  465.3 0.7 copy-done.1
  466.0 3.4 fusion.10
  469.4 48.7 %psum.23 = f32[8,512]{1,0:T(8,128)S(1)} all-reduce(f32[8,512]{1,0:T(8,128)S(1)} %fusion.10), channel_id=1, replica_groups=mesh['row'=2,'col'=64] {'row'}, use_global_device_ids=true, to_apply=%region_2.3 | all-reduce | flops 4096 | bytes 32768 | tf_op jit(solution)/shard_map/psum | solution.py:47
  518.1 0.6 broadcast_multiply_fusion
  518.7 1.5 convert_element_type.42
  (17 shorter events, 0.2 us)
Async XLA Ops:
  7.2 107.7 %copy-start = (bf16[8,512]{1,0:T(8,128)(2,1)S(1)}, bf16[8,512]{1,0:T(8,128)(2,1)}, u32[]{:S(2)}) copy-start(bf16[8,512]{1,0:T(8,128)(2,1)} %param.10) | copy-start | bytes 24580
  7.2 31.0 %all-reduce.3.cloned.1.call-start = ((), (), s32[]{:S(2)}) async-start(), calls=%async_computation.5 | async-start | bytes 262144 | tf_op jit(solution)/shard_map/psum | solution.py:9
  8.8 106.1 %all-gather.2.cloned.1.call-start = ((), (), s32[]{:S(2)}) async-start(), calls=%async_computation.2 | async-start | bytes 4259840 | tf_op jit(solution)/shard_map/all_gather | solution.py:37
  43.4 74.9 %copy-start.2 = (bf16[8,4096]{1,0:T(8,128)(2,1)S(1)}, bf16[8,4096]{1,0:T(8,128)(2,1)}, u32[]{:S(2)}) copy-start(bf16[8,4096]{1,0:T(8,128)(2,1)} %param.11) | copy-start | bytes 196612
  46.4 409.7 %reduce-scatter.7.cloned.1.call-start = ((), (), s32[]{:S(2)}) async-start(), calls=%async_computation.4 | async-start | bytes 8519680
  131.8 0.7 copy-start.3
  131.9 386.9 %reduce-scatter.5.cloned.1.call-start = ((), (), s32[]{:S(2)}) async-start(), calls=%async_computation.3 | async-start | bytes 393216 | tf_op jit(solution)/shard_map/reduce_scatter | solution.py:66
  465.3 0.7 copy-start.1
Sparse Core Ops, SparseCore 0:
  11.0 27.1 all-reduce.2
  46.5 68.3 all-gather.1
  132.0 323.9 reduce-scatter.6
  466.2 50.4 reduce-scatter.4
where the time goes:
time: 528 us; the launch traced here: 527 us
  waiting for transfers between devices  415 us (79%)
  blocking collectives  48.7 us (9%)
  matrix products  19.4 us (4%)
  local copies, waits for them, and re-layouts  15.3 us (3%)
  other arithmetic  14.6 us (3%)
  between operations  13.8 us (3%)
    unnamed x5, waiting for transfers between devices  323 us
    all_gather x1, waiting for transfers between devices, local(): agg_full = lax.all_gather(aggregated, 'col', axis=0, tiled=True)  68.5 us
    psum x1, blocking collectives, local(): lax.psum(local_grad, 'row') / jnp.sqrt(jnp.float32(node_total))  48.7 us
    psum x1, waiting for transfers between devices, from_root(): return lax.psum(kept, axis)  23 us
    unnamed x10, local copies, waits for them, and re-layouts  11.7 us
  transfers between devices with their start and end apart: 4, of which 3 were waited for; matrix products, arithmetic and copies ran while one was open for 2% of the time, Pallas kernels for 0%

commit v1 on v0

v1 whole, which is shorter than its diff:
```python
import functools

import jax
import jax.numpy as jnp
from jax import lax
from jax.experimental import pallas as pl
from jax.experimental.pallas import tpu as pltpu
from jax.sharding import PartitionSpec as P

STEPS = 4
SWAP = [(0, 1), (1, 0)]


def lower_half(shape):
    return lax.broadcasted_iota(jnp.int32, shape, len(shape) - 1) < shape[-1] // 2


def halves(a, b):
    mask = lower_half(a.shape)
    half = a.shape[-1] // 2
    return (
        jnp.where(mask, a, pltpu.roll(b, half, a.ndim - 1)),
        jnp.where(mask, pltpu.roll(a, half, a.ndim - 1), b),
    )


def gather_kernel(cols, counts, own, other, a_ref, weight, cot, msg, feats):
    step = pl.program_id(0)
    per = a_ref.shape[0]
    row = lax.axis_index("row")

    @pl.when(step == 0)
    def _():
        feats[row] = own[...]
        feats[1 - row] = other[...]

    for i in range(per):
        b = step * per + i
        total = jnp.zeros((8, 128), jnp.float32)
        for s in range(2):
            for k in range(2):
                col = pl.multiple_of(cols[b, s * 2 + k] * 128, 128)
                x = feats[s, :, pl.ds(col, 128)]
                x = lax.select(k < counts[b, s], x, jnp.zeros_like(x))
                total += lax.dot_general(
                    x, a_ref[i, s, k], (((1,), (1,)), ((), ())), preferred_element_type=jnp.float32
                )
        first, second = halves(total, cot[:, i * 128 : (i + 1) * 128].astype(jnp.float32))
        msg[2 * i, :, :128] = first.astype(jnp.bfloat16)
        msg[2 * i + 1, :, :128] = second.astype(jnp.bfloat16)
    w = weight[...]
    for i in range(2 * per):
        msg[i, :, 128:] = w


def dense_kernel(msg, back):
    w = msg[:, 128:]
    pair = msg[:, :128]
    pre = jnp.dot(w, pair, preferred_element_type=jnp.float32)
    cot = pltpu.roll(pair.astype(jnp.float32), 64, 1)
    sig = jax.nn.sigmoid(pre)
    out = pre * sig
    dpre = cot * sig * (1.0 + pre * (1.0 - sig))
    dpre = jnp.where(lower_half(dpre.shape), dpre, 0.0).astype(jnp.bfloat16)
    dagg = lax.dot_general(w, dpre, (((0,), (0,)), ((), ())), preferred_element_type=jnp.float32)
    back[:, :128] = jnp.where(lower_half(out.shape), out, pltpu.roll(dagg, 64, 1)).astype(jnp.bfloat16)
    grad = lax.dot_general(dpre, pair, (((1,), (1,)), ((), ())), preferred_element_type=jnp.float32)
    back[:, 128:] = grad.astype(jnp.bfloat16)


def scatter_kernel(cols, counts, back, a_ref, out, own, send, terms, grad):
    step = pl.program_id(0)
    per = a_ref.shape[0]
    row = lax.axis_index("row")

    @pl.when(step == 0)
    def _():
        terms[...] = jnp.zeros_like(terms)
        grad[...] = jnp.zeros_like(grad)

    part = jnp.zeros(grad.shape, jnp.float32)
    for i in range(2 * per):
        part += back[i, :, 128:].astype(jnp.float32)
    grad[...] += part
    for i in range(per):
        b = step * per + i
        outs, dagg = halves(
            back[2 * i, :, :128].astype(jnp.float32), back[2 * i + 1, :, :128].astype(jnp.float32)
        )
        out[:, i * 128 : (i + 1) * 128] = outs.astype(jnp.bfloat16)
        dagg = dagg.astype(jnp.bfloat16)
        for s in range(2):
            for k in range(2):
                col = pl.multiple_of(cols[b, s * 2 + k] * 128, 128)
                term = jnp.dot(dagg, a_ref[i, s, k], preferred_element_type=jnp.float32)
                term = lax.select(k < counts[b, s], term, jnp.zeros_like(term))
                terms[s, :, pl.ds(col, 128)] += term

    @pl.when(step == pl.num_programs(0) - 1)
    def _():
        own[:, :4096] = terms[row]
        own[:, 4096:] = grad[...]
        send[:, :4096] = terms[1 - row]
        send[:, 4096:] = grad[...]


def merge_kernel(scale, own, other, grad_features, grad_weight):
    total = own[...] + other[...]
    grad_features[...] = total[:, :4096].astype(jnp.bfloat16)
    grad_weight[...] = total[:, 4096:] * scale


def local(features, a_blocks, block_cols, block_counts, weight, cotangent):
    fd, slab = features.shape
    nb = a_blocks.shape[0]
    width = weight.shape[1]
    col = lax.axis_size("col")
    per = nb // STEPS
    smem = pl.BlockSpec(memory_space=pltpu.SMEM)
    cols = block_cols.reshape(nb, 4)
    a_spec = pl.BlockSpec((per, 2, 2, 128, 128), lambda t: (t, 0, 0, 0, 0))
    whole = lambda *shape: pl.BlockSpec(shape, lambda t: (0,) * len(shape))
    msg_spec = pl.BlockSpec((2 * per, fd, 128 + width), lambda t: (t, 0, 0))
    lanes = pl.BlockSpec((fd, per * 128), lambda t: (0, t))

    other = lax.ppermute(features, "row", SWAP)
    msg = pl.pallas_call(
        gather_kernel,
        grid=(STEPS,),
        in_specs=[smem, smem, whole(fd, slab), whole(fd, slab), a_spec, whole(fd, width), lanes],
        out_specs=msg_spec,
        out_shape=jax.ShapeDtypeStruct((col, fd, 128 + width), jnp.bfloat16),
        scratch_shapes=[pltpu.VMEM((2, fd, slab), jnp.bfloat16)],
        name="gather",
    )(cols, block_counts, features, other, a_blocks, weight, cotangent)
    msg = lax.all_to_all(msg.reshape(col * fd, 128 + width), "col", 0, 0, tiled=True)
    back = pl.pallas_call(
        dense_kernel,
        out_shape=jax.ShapeDtypeStruct(msg.shape, jnp.bfloat16),
        name="dense",
    )(msg)
    back = lax.all_to_all(back, "col", 0, 0, tiled=True).reshape(col, fd, 128 + width)
    part = jax.ShapeDtypeStruct((fd, slab + width), jnp.float32)
    output, own, send = pl.pallas_call(
        scatter_kernel,
        grid=(STEPS,),
        in_specs=[smem, smem, msg_spec, a_spec],
        out_specs=[lanes, whole(fd, slab + width), whole(fd, slab + width)],
        out_shape=[jax.ShapeDtypeStruct((fd, slab), jnp.bfloat16), part, part],
        scratch_shapes=[pltpu.VMEM((2, fd, slab), jnp.float32), pltpu.VMEM((fd, width), jnp.float32)],
        name="scatter",
    )(cols, block_counts, back, a_blocks)
    got = lax.ppermute(send, "row", SWAP)
    scale = 1.0 / (slab * lax.axis_size("row")) ** 0.5
    grad_features, grad_weight = pl.pallas_call(
        functools.partial(merge_kernel, scale),
        out_shape=[
            jax.ShapeDtypeStruct((fd, slab), jnp.bfloat16),
            jax.ShapeDtypeStruct((fd, width), jnp.float32),
        ],
        name="merge",
    )(own, got)
    return output, grad_weight, grad_features


def solution(mesh):
    placed = (
        P("col", "row"),
        P("row", None, None, None, None),
        P("row", None, None),
        P("row", None),
        P("col", None),
        P("col", "row"),
    )
    return jax.shard_map(
        local,
        mesh=mesh,
        in_specs=placed,
        out_specs=(P("col", "row"), P("col", None), P("col", "row")),
        check_vma=False,
    )
```

time: 528 us -> 69.5 us (0.13)
  waiting for transfers between devices: 415 us -> 1.22 us
  matrix products: 19.4 us -> 0 us
  Pallas kernels: 0 us -> 15 us
  other arithmetic: 14.6 us -> 0 us
  between operations: 13.8 us -> 0.64 us
  local copies, waits for them, and re-layouts: 15.3 us -> 4 us
    unnamed x5 -> x0, waiting for transfers between devices: 323 us -> none
    all_gather x1 -> x0, waiting for transfers between devices: 68.5 us -> none  [local(): agg_full = lax.all_gather(aggregated, 'col', axis=0, tiled=True)]
    psum x1 -> x0, blocking collectives: 48.7 us -> none  [local(): lax.psum(local_grad, 'row') / jnp.sqrt(jnp.float32(node_total))]
    all_to_all x0 -> x2, blocking collectives: none -> 43.9 us  [the longest x1 25.5 us: local(): lax.all_to_all(msg.reshape(col * fd, 128 + width), 'col', 0, 0, tiled=True)]
    psum x1 -> x0, waiting for transfers between devices: 23 us -> none  [from_root(): return lax.psum(kept, axis)]
    dot_general x6 -> x0, matrix products: 19.4 us -> none  [the longest x2 5.14 us: local(): jnp.einsum('fbkj,bkij->fbi', picked, masked[:, section_idx], preferred_el...]
    pallas_call x0 -> x4, Pallas kernels: none -> 15 us  [the longest x1 5.6 us: local(): pl.pallas_call(gather_kernel, grid=(STEPS,), in_specs=[smem, smem, whole(...]
    unnamed x10 -> x5, local copies, waits for them, and re-layouts: 11.7 us -> 2.64 us
  transfers between devices with their start and end apart: 4 -> 2, of which waited for: 3 -> 1; matrix products, arithmetic and copies ran while one was open for 2% -> 4% of each run, Pallas kernels for 0% -> 0%
where the time goes in v1:
time: 69.5 us; the launch traced here: 69 us
  blocking collectives  43.9 us (63%)
  Pallas kernels  15 us (22%)
  starting transfers between devices  4.15 us (6%)
  local copies, waits for them, and re-layouts  4 us (6%)
  waiting for transfers between devices  1.22 us (2%)
    all_to_all x1, blocking collectives, local(): lax.all_to_all(msg.reshape(col * fd, 128 + width), 'col', 0, 0, tiled=True)  25.5 us
    all_to_all x1, blocking collectives, local(): lax.all_to_all(back, 'col', 0, 0, tiled=True).reshape(col, fd, 128 + width)  18.4 us
    pallas_call x1, Pallas kernels, local(): pl.pallas_call(gather_kernel, grid=(STEPS,), in_specs=[smem, smem, whole(...  5.6 us
    pallas_call x1, Pallas kernels, local(): pl.pallas_call(scatter_kernel, grid=(STEPS,), in_specs=[smem, smem, msg_s...  4.98 us
    pallas_call x1, Pallas kernels, local(): pl.pallas_call(dense_kernel, out_shape=jax.ShapeDtypeStruct(msg.shape, jn...  2.81 us
    ppermute x1, starting transfers between devices, local(): got = lax.ppermute(send, 'row', SWAP)  2.69 us
    unnamed x5, local copies, waits for them, and re-layouts  2.64 us
    pallas_call x1, Pallas kernels, local(): pl.pallas_call(functools.partial(merge_kernel, scale), out_shape=[jax.Sha...  1.63 us
  transfers between devices with their start and end apart: 2, of which 1 were waited for; matrix products, arithmetic and copies ran while one was open for 4% of the time, Pallas kernels for 0%

profile of v1, /device:TPU:1, one launch (start us, length us, event | category | flops | bytes accessed | tf_op | source)
XLA Modules:
  0.0 69.0 jit_solution(3394175127952347844)
XLA Ops:
  0.6 1.5 %collective-permute-start = (bf16[8,4096]{1,0:T(8,128)(2,1)}, bf16[8,4096]{1,0:T(8,128)(2,1)S(1)}, u32[]{:S(2)}, u32[]{:S(2)}) collective-permute-start(bf16[8,4096]{1,0:T(8,128)(2,1)} %own.1), channel_id=1, source_target_pairs={{0,64},{64,0},{1,65},{65,1},{2,66},{66,2},{3,67},{67,3},{4,68},{68... | collective-permute-start | bytes 196616 | tf_op jit(solution)/shard_map/ppermute | solution.py:126
  2.1 1.4 %copy.11.cols = s32[32,4]{1,0:T(8,128)} copy(s32[32,4]{0,1:T(4,128)} %bitcast.5) | data formatting | bytes 1024 | tf_op jit(solution)/shard_map/reshape | solution.py:120
  3.5 1.4 %copy.12.counts = s32[32,2]{1,0:T(8,128)} copy(s32[32,2]{0,1:T(2,128)} %param.9) | data formatting | bytes 512 | tf_op args[3]
  4.8 0.0 collective-permute-done.other
  4.8 0.0 copy-start.1
  4.8 0.6 copy-done.1
  5.4 5.6 %gather.1 = bf16[64,8,640]{2,1,0:T(8,128)(2,1)} custom-call(s32[32,4]{1,0:T(8,128)} %copy.11.cols, s32[32,2]{1,0:T(8,128)} %copy.12.counts, bf16[8,4096]{1,0:T(8,128)(2,1)} %own.1, bf16[8,4096]{1,0:T(8,128)(2,1)} %copy-done.1, bf16[32,2,2,128,128]{4,3,2,1,0:T(8,128)(2,1)} %a_ref.3, bf16[8,512]{1,0:T(8,128)(2,1)} %weight.1, bf16[8,4096]{1,0:T(8,128)(2,1)} %cot.1), custom_call_target="tpu_custom_call" | custom-call | tf_op jit(solution)/shard_map/gather/pallas_call | solution.py:127
  11.1 25.5 %all_to_all.17 = bf16[64,8,640]{2,1,0:T(8,128)(2,1)} all-to-all(bf16[64,8,640]{2,1,0:T(8,128)(2,1)} %gather.1), channel_id=1, replica_groups=mesh['row'=2,'col'=64] {'col'}, dimensions={0} | all-to-all | bytes 1310720 | tf_op jit(solution)/shard_map/all_to_all | solution.py:136
  36.5 2.8 %dense.1 = bf16[512,640]{1,0:T(8,128)(2,1)} custom-call(bf16[512,640]{1,0:T(8,128)(2,1)} %bitcast.3), custom_call_target="tpu_custom_call" | custom-call | tf_op jit(solution)/shard_map/dense/pallas_call | solution.py:137
  39.4 18.4 %all_to_all.18.back = bf16[64,8,640]{2,1,0:T(8,128)(2,1)} all-to-all(bf16[64,8,640]{2,1,0:T(8,128)(2,1)} %bitcast.4), channel_id=1, replica_groups=mesh['row'=2,'col'=64] {'col'}, dimensions={0} | all-to-all | bytes 1310720 | tf_op jit(solution)/shard_map/all_to_all | solution.py:142
  57.8 5.0 %scatter.1 = (bf16[8,4096]{1,0:T(8,128)(2,1)}, f32[8,4608]{1,0:T(8,128)}, f32[8,4608]{1,0:T(8,128)}) custom-call(s32[32,4]{1,0:T(8,128)} %copy.11.cols, s32[32,2]{1,0:T(8,128)} %copy.12.counts, bf16[64,8,640]{2,1,0:T(8,128)(2,1)} %all_to_all.18.back, bf16[32,2,2,128,128]{4,3,2,1,0:T(8,128)(2,1)} %a_ref.3), custom_call_target="tpu_custom_call" | custom-call | tf_op jit(solution)/shard_map/scatter/pallas_call | solution.py:144
  62.8 2.7 %collective-permute-start.1 = (f32[8,4608]{1,0:T(8,128)}, f32[8,4608]{1,0:T(8,128)S(1)}, u32[]{:S(2)}, u32[]{:S(2)}) collective-permute-start(f32[8,4608]{1,0:T(8,128)} %get-tuple-element.10), channel_id=1, source_target_pairs={{0,64},{64,0},{1,65},{65,1},{2,66},{66,2},{3,67},{67,3},{4,68},{68... | collective-permute-start | bytes 442376 | tf_op jit(solution)/shard_map/ppermute | solution.py:153
  65.5 1.2 %collective-permute-done.1.other = f32[8,4608]{1,0:T(8,128)S(1)} collective-permute-done((f32[8,4608]{1,0:T(8,128)}, f32[8,4608]{1,0:T(8,128)S(1)}, u32[]{:S(2)}, u32[]{:S(2)}) %collective-permute-start.1) | collective-permute-done | bytes 147488 | tf_op jit(solution)/shard_map/ppermute | solution.py:153
  66.7 0.0 copy-start
  66.7 0.6 copy-done
  67.3 1.6 %merge.1 = (bf16[8,4096]{1,0:T(8,128)(2,1)}, f32[8,512]{1,0:T(8,128)}) custom-call(f32[8,4608]{1,0:T(8,128)} %get-tuple-element.9.own, f32[8,4608]{1,0:T(8,128)} %copy-done), custom_call_target="tpu_custom_call" | custom-call | tf_op jit(solution)/shard_map/merge/pallas_call | solution.py:155
Async XLA Ops:
  0.6 4.2 %collective-permute-start = (bf16[8,4096]{1,0:T(8,128)(2,1)}, bf16[8,4096]{1,0:T(8,128)(2,1)S(1)}, u32[]{:S(2)}, u32[]{:S(2)}) collective-permute-start(bf16[8,4096]{1,0:T(8,128)(2,1)} %own.1), channel_id=1, source_target_pairs={{0,64},{64,0},{1,65},{65,1},{2,66},{66,2},{3,67},{67,3},{4,68},{68... | collective-permute-start | bytes 196616 | tf_op jit(solution)/shard_map/ppermute | solution.py:126
  4.8 0.6 copy-start.1
  62.8 3.9 %collective-permute-start.1 = (f32[8,4608]{1,0:T(8,128)}, f32[8,4608]{1,0:T(8,128)S(1)}, u32[]{:S(2)}, u32[]{:S(2)}) collective-permute-start(f32[8,4608]{1,0:T(8,128)} %get-tuple-element.10), channel_id=1, source_target_pairs={{0,64},{64,0},{1,65},{65,1},{2,66},{66,2},{3,67},{67,3},{4,68},{68... | collective-permute-start | bytes 442376 | tf_op jit(solution)/shard_map/ppermute | solution.py:153
  66.7 0.7 copy-start

commit v2 on v0

v2 whole, which is shorter than its diff:
```python
import functools

import jax
import jax.numpy as jnp
from jax import lax
from jax.experimental import pallas as pl
from jax.experimental.pallas import tpu as pltpu
from jax.sharding import PartitionSpec as P

SWAP = [(0, 1), (1, 0)]
VMEM_LIMIT = 4 << 20
CHUNKS = 4


def lower_half(shape):
    return lax.broadcasted_iota(jnp.int32, shape, len(shape) - 1) < shape[-1] // 2


def halves(a, b):
    mask = lower_half(a.shape)
    half = a.shape[-1] // 2
    return (
        jnp.where(mask, a, pltpu.roll(b, half, a.ndim - 1)),
        jnp.where(mask, pltpu.roll(a, half, a.ndim - 1), b),
    )


def first_kernel(cols_hbm, counts_hbm, own_hbm, a_hbm, a_ref, total, own, cols, counts, sems):
    row = lax.axis_index("row")
    blocks = a_ref.shape[0]
    per = blocks // CHUNKS
    small = [
        pltpu.make_async_copy(src, dst, sems.at[i])
        for i, (src, dst) in enumerate(((cols_hbm, cols), (counts_hbm, counts), (own_hbm, own)))
    ]
    large = [
        pltpu.make_async_copy(
            a_hbm.at[pl.ds(c * per, per)], a_ref.at[pl.ds(c * per, per)], sems.at[len(small) + c]
        )
        for c in range(CHUNKS)
    ]
    for copy in small + large:
        copy.start()
    for copy in small:
        copy.wait()
    for b in range(blocks):
        if b % per == 0:
            large[b // per].wait()
        total[:, b * 128 : (b + 1) * 128] = aggregate(cols, counts, own, a_ref, row, b)


def aggregate(cols, counts, feats, a_ref, s, b):
    total = jnp.zeros((8, 128), jnp.float32)
    for k in range(2):
        col = pl.multiple_of(cols[s, k, b] * 128, 128)
        x = feats[:, pl.ds(col, 128)]
        x = lax.select(k < counts[s, b], x, jnp.zeros_like(x))
        total += lax.dot_general(
            x, a_ref[b, s, k], (((1,), (1,)), ((), ())), preferred_element_type=jnp.float32
        )
    return total


def second_kernel(cols, counts, other, a_ref, part, weight, cot, msg):
    row = lax.axis_index("row")
    for b in range(a_ref.shape[0]):
        here = slice(b * 128, (b + 1) * 128)
        total = part[:, here] + aggregate(cols, counts, other, a_ref, 1 - row, b)
        total = total.astype(jnp.bfloat16).astype(jnp.float32)
        first, second = halves(total, cot[:, here].astype(jnp.float32))
        msg[2 * b, :, :128] = first.astype(jnp.bfloat16)
        msg[2 * b + 1, :, :128] = second.astype(jnp.bfloat16)
    w = weight[...]
    for b in range(msg.shape[0]):
        msg[b, :, 128:] = w


def dense_kernel(msg, back):
    w = msg[:, 128:]
    pair = msg[:, :128]
    pre = jnp.dot(w, pair, preferred_element_type=jnp.float32)
    cot = pltpu.roll(pair.astype(jnp.float32), 64, 1)
    sig = jax.nn.sigmoid(pre)
    out = pre * sig
    dpre = cot * sig * (1.0 + pre * (1.0 - sig))
    dpre = jnp.where(lower_half(dpre.shape), dpre, 0.0).astype(jnp.bfloat16)
    dagg = lax.dot_general(w, dpre, (((0,), (0,)), ((), ())), preferred_element_type=jnp.float32)
    back[:, :128] = jnp.where(lower_half(out.shape), out, pltpu.roll(dagg, 64, 1)).astype(jnp.bfloat16)
    grad = lax.dot_general(dpre, pair, (((1,), (1,)), ((), ())), preferred_element_type=jnp.float32)
    back[:, 128:] = grad.astype(jnp.bfloat16)


def spread(cols, counts, dagg, a_ref, s, b, terms):
    for k in range(2):
        col = pl.multiple_of(cols[s, k, b] * 128, 128)
        term = jnp.dot(dagg, a_ref[b, s, k], preferred_element_type=jnp.float32)
        term = lax.select(k < counts[s, b], term, jnp.zeros_like(term))
        terms[:, pl.ds(col, 128)] += term


def send_kernel(cols, counts, back, a_ref, send, dagg_ref):
    row = lax.axis_index("row")
    blocks = a_ref.shape[0]
    slab = blocks * 128
    send[...] = jnp.zeros_like(send)
    for b in range(blocks):
        _, dagg = halves(
            back[2 * b, :, :128].astype(jnp.float32), back[2 * b + 1, :, :128].astype(jnp.float32)
        )
        dagg = dagg.astype(jnp.bfloat16)
        dagg_ref[:, b * 128 : (b + 1) * 128] = dagg
        spread(cols, counts, dagg, a_ref, 1 - row, b, send)
    grad = jnp.zeros((send.shape[0], send.shape[1] - slab), jnp.float32)
    for b in range(2 * blocks):
        grad += back[b, :, 128:].astype(jnp.float32)
    send[:, slab:] = grad


def keep_kernel(cols, counts, back, a_ref, dagg_ref, out, own):
    row = lax.axis_index("row")
    own[...] = jnp.zeros_like(own)
    for b in range(a_ref.shape[0]):
        here = slice(b * 128, (b + 1) * 128)
        outs, _ = halves(
            back[2 * b, :, :128].astype(jnp.float32), back[2 * b + 1, :, :128].astype(jnp.float32)
        )
        out[:, here] = outs.astype(jnp.bfloat16)
        spread(cols, counts, dagg_ref[:, here], a_ref, row, b, own)


def merge_kernel(scale, own, sent, got, grad_features, grad_weight):
    slab = own.shape[1]
    grad_features[...] = (own[...] + got[:, :slab]).astype(jnp.bfloat16)
    grad_weight[...] = (sent[:, slab:] + got[:, slab:]) * scale


def call(kernel, name, scalars, arrays, outs):
    vmem = pl.BlockSpec(memory_space=pltpu.VMEM)
    smem = pl.BlockSpec(memory_space=pltpu.SMEM)
    return pl.pallas_call(
        kernel,
        in_specs=[smem] * len(scalars) + [vmem] * len(arrays),
        out_specs=[vmem] * len(outs),
        out_shape=[jax.ShapeDtypeStruct(shape, dtype) for shape, dtype in outs],
        compiler_params=pltpu.CompilerParams(vmem_limit_bytes=VMEM_LIMIT),
        name=name,
    )(*scalars, *arrays)


def local(features, a_blocks, block_cols, block_counts, weight, cotangent):
    fd, slab = features.shape
    width = weight.shape[1]
    ranks = lax.axis_size("col")
    scalars = (block_cols.transpose(1, 2, 0), block_counts.transpose(1, 0))
    bf16, f32 = jnp.bfloat16, jnp.float32

    other = lax.ppermute(features, "row", SWAP)
    hbm = pl.BlockSpec(memory_space=pltpu.HBM)
    vmem = pl.BlockSpec(memory_space=pltpu.VMEM)
    smem = pl.BlockSpec(memory_space=pltpu.SMEM)
    a_blocks, part = pl.pallas_call(
        first_kernel,
        in_specs=[hbm] * 4,
        out_specs=[vmem, vmem],
        out_shape=[
            jax.ShapeDtypeStruct(a_blocks.shape, bf16),
            jax.ShapeDtypeStruct((fd, slab), f32),
        ],
        scratch_shapes=[
            pltpu.VMEM(features.shape, bf16),
            pltpu.SMEM(scalars[0].shape, jnp.int32),
            pltpu.SMEM(scalars[1].shape, jnp.int32),
            pltpu.SemaphoreType.DMA((3 + CHUNKS,)),
        ],
        compiler_params=pltpu.CompilerParams(vmem_limit_bytes=VMEM_LIMIT),
        name="first",
    )(*(pltpu.with_memory_space_constraint(x, pltpu.HBM) for x in (*scalars, features, a_blocks)))
    (msg,) = call(
        second_kernel,
        "second",
        scalars,
        (other, a_blocks, part, weight, cotangent),
        [((ranks, fd, 128 + width), bf16)],
    )
    msg = lax.all_to_all(msg.reshape(ranks * fd, 128 + width), "col", 0, 0, tiled=True)
    (back,) = call(dense_kernel, "dense", (), (msg,), [(msg.shape, bf16)])
    back = lax.all_to_all(back, "col", 0, 0, tiled=True).reshape(ranks, fd, 128 + width)
    send, dagg = call(
        send_kernel,
        "send",
        scalars,
        (back, a_blocks),
        [((fd, slab + width), f32), ((fd, slab), bf16)],
    )
    got = lax.ppermute(send, "row", SWAP)
    output, own = call(
        keep_kernel,
        "keep",
        scalars,
        (back, a_blocks, dagg),
        [((fd, slab), bf16), ((fd, slab), f32)],
    )
    scale = 1.0 / (slab * lax.axis_size("row")) ** 0.5
    grad_features, grad_weight = call(
        functools.partial(merge_kernel, scale),
        "merge",
        (),
        (own, send, got),
        [((fd, slab), bf16), ((fd, width), f32)],
    )
    return output, grad_weight, grad_features


def solution(mesh):
    placed = (
        P("col", "row"),
        P("row", None, None, None, None),
        P("row", None, None),
        P("row", None),
        P("col", None),
        P("col", "row"),
    )
    return jax.shard_map(
        local,
        mesh=mesh,
        in_specs=placed,
        out_specs=(P("col", "row"), P("col", None), P("col", "row")),
        check_vma=False,
    )
```

time: 528 us -> 56.9 us (0.11)
  waiting for transfers between devices: 415 us -> 0.01 us
  matrix products: 19.4 us -> 0 us
  local copies, waits for them, and re-layouts: 15.3 us -> 0.02 us
  other arithmetic: 14.6 us -> 0 us
  between operations: 13.8 us -> 0.72 us
  Pallas kernels: 0 us -> 9.37 us
  blocking collectives: 48.7 us -> 42.1 us
    unnamed x5 -> x0, waiting for transfers between devices: 323 us -> none
    all_gather x1 -> x0, waiting for transfers between devices: 68.5 us -> none  [local(): agg_full = lax.all_gather(aggregated, 'col', axis=0, tiled=True)]
    psum x1 -> x0, blocking collectives: 48.7 us -> none  [local(): lax.psum(local_grad, 'row') / jnp.sqrt(jnp.float32(node_total))]
    all_to_all x0 -> x2, blocking collectives: none -> 42.1 us  [the longest x1 25.2 us: local(): lax.all_to_all(msg.reshape(ranks * fd, 128 + width), 'col', 0, 0, tiled=T...]
    psum x1 -> x0, waiting for transfers between devices: 23 us -> none  [from_root(): return lax.psum(kept, axis)]
    dot_general x6 -> x0, matrix products: 19.4 us -> none  [the longest x2 5.14 us: local(): jnp.einsum('fbkj,bkij->fbi', picked, masked[:, section_idx], preferred_el...]
    unnamed x10 -> x8, local copies, waits for them, and re-layouts: 11.7 us -> 0.02 us
    pallas_call x0 -> x6, Pallas kernels: none -> 9.37 us  [the longest x5 6.5 us: call(): pl.pallas_call(kernel, in_specs=[smem] * len(scalars) + [vmem] * len(arra...]
  transfers between devices with their start and end apart: 4 -> 2, of which waited for: 3 -> 0; matrix products, arithmetic and copies ran while one was open for 2% -> 0% of each run, Pallas kernels for 0% -> 8%
where the time goes in v2:
time: 56.9 us; the launch traced here: 56.7 us
  blocking collectives  42.1 us (74%)
  Pallas kernels  9.37 us (16%)
  starting transfers between devices  4.49 us (8%)
  between operations  0.72 us (1%)
    all_to_all x1, blocking collectives, local(): lax.all_to_all(msg.reshape(ranks * fd, 128 + width), 'col', 0, 0, tiled=T...  25.2 us
    all_to_all x1, blocking collectives, local(): lax.all_to_all(back, 'col', 0, 0, tiled=True)  16.9 us
    pallas_call x5, Pallas kernels, call(): pl.pallas_call(kernel, in_specs=[smem] * len(scalars) + [vmem] * len(arra...  6.5 us
    ppermute x1, starting transfers between devices, local(): got = lax.ppermute(send, 'row', SWAP)  3.03 us
    pallas_call x1, Pallas kernels, local(): pl.pallas_call(first_kernel, in_specs=[hbm] * 4, out_specs=[vmem, vmem],...  2.87 us
    ppermute x1, starting transfers between devices, local(): other = lax.ppermute(features, 'row', SWAP)  1.46 us
  transfers between devices with their start and end apart: 2, of which 0 were waited for; matrix products, arithmetic and copies ran while one was open for 0% of the time, Pallas kernels for 8%

profile of v2, /device:TPU:1, one launch (start us, length us, event | category | flops | bytes accessed | tf_op | source)
XLA Modules:
  0.0 56.7 jit_solution(13531267843609904024)
XLA Ops:
  0.6 0.0 copy-start.2
  0.6 0.0 copy-start.1
  0.7 0.0 copy-start
  0.7 0.0 copy-start.3
  0.7 1.5 %collective-permute-start = (bf16[8,4096]{1,0:T(8,128)(2,1)}, bf16[8,4096]{1,0:T(8,128)(2,1)S(1)}, u32[]{:S(2)}, u32[]{:S(2)}) collective-permute-start(bf16[8,4096]{1,0:T(8,128)(2,1)} %own_hbm.1), channel_id=1, source_target_pairs={{0,64},{64,0},{1,65},{65,1},{2,66},{66,2},{3,67},{67,3},{4,68},{68... | collective-permute-start | bytes 196616 | tf_op jit(solution)/shard_map/ppermute | solution.py:157
  2.1 2.9 %first.1 = (bf16[32,2,2,128,128]{4,3,2,1,0:T(8,128)(2,1)S(1)}, f32[8,4096]{1,0:T(8,128)S(1)}) custom-call(s32[2,2,32]{2,1,0:T(2,128)} %bitcast.6, s32[2,32]{1,0:T(2,128)} %bitcast.10, bf16[8,4096]{1,0:T(8,128)(2,1)} %own_hbm.1, bf16[32,2,2,128,128]{4,3,2,1,0:T(8,128)(2,1)} %a_hbm.1), custom_call_target="tpu_custom_call" | custom-call | tf_op jit(solution)/shard_map/first/pallas_call | solution.py:161
  5.0 0.0 collective-permute-done.other
  5.0 0.0 copy-done.2
  5.0 0.0 copy-done.1
  5.0 0.0 copy-done
  5.1 0.0 copy-done.3
  5.1 1.9 %second.1 = bf16[64,8,640]{2,1,0:T(8,128)(2,1)S(1)} custom-call(s32[2,2,32]{2,1,0:T(2,128)S(1)} %bitcast.7, s32[2,32]{1,0:T(2,128)S(1)} %bitcast.11, bf16[8,4096]{1,0:T(8,128)(2,1)S(1)} %collective-permute-done.other, bf16[32,2,2,128,128]{4,3,2,1,0:T(8,128)(2,1)S(1)} %get-tuple-element.11.a_ref, f32[8,4096]{1,0:T(8,128)S(1)} %get-tuple-element.12.part, ...), custom_call_target="tpu_custom_call" | custom-call | tf_op jit(solution)/shard_map/second/pallas_call | solution.py:140
  6.9 25.2 %all_to_all.17 = bf16[64,8,640]{2,1,0:T(8,128)(2,1)S(1)} all-to-all(bf16[64,8,640]{2,1,0:T(8,128)(2,1)S(1)} %second.1), channel_id=1, replica_groups=mesh['row'=2,'col'=64] {'col'}, dimensions={0} | all-to-all | bytes 1310720 | tf_op jit(solution)/shard_map/all_to_all | solution.py:185
  32.1 0.9 %dense.1 = bf16[512,640]{1,0:T(8,128)(2,1)S(1)} custom-call(bf16[512,640]{1,0:T(8,128)(2,1)S(1)} %bitcast.4), custom_call_target="tpu_custom_call" | custom-call | tf_op jit(solution)/shard_map/dense/pallas_call | solution.py:140
  33.0 16.9 %all_to_all.18.back = bf16[64,8,640]{2,1,0:T(8,128)(2,1)S(1)} all-to-all(bf16[64,8,640]{2,1,0:T(8,128)(2,1)S(1)} %bitcast.5), channel_id=1, replica_groups=mesh['row'=2,'col'=64] {'col'}, dimensions={0} | all-to-all | bytes 1310720 | tf_op jit(solution)/shard_map/all_to_all | solution.py:187
  49.9 1.3 %send.1 = (f32[8,4608]{1,0:T(8,128)S(1)}, bf16[8,4096]{1,0:T(8,128)(2,1)S(1)}) custom-call(s32[2,2,32]{2,1,0:T(2,128)S(1)} %bitcast.8, s32[2,32]{1,0:T(2,128)S(1)} %bitcast.12, bf16[64,8,640]{2,1,0:T(8,128)(2,1)S(1)} %all_to_all.18.back, bf16[32,2,2,128,128]{4,3,2,1,0:T(8,128)(2,1)S(1)} %get-tuple-element.11.a_ref), custom_call_target="tpu_custom_call" | custom-call | tf_op jit(solution)/shard_map/send/pallas_call | solution.py:140
  51.2 3.0 %collective-permute-start.1 = (f32[8,4608]{1,0:T(8,128)S(1)}, f32[8,4608]{1,0:T(8,128)S(1)}, u32[]{:S(2)}, u32[]{:S(2)}) collective-permute-start(f32[8,4608]{1,0:T(8,128)S(1)} %get-tuple-element.16.sent), channel_id=1, source_target_pairs={{0,64},{64,0},{1,65},{65,1},{2,66},{66,2},{3,67},{67,3},{4,68},{68... | collective-permute-start | bytes 442376 | tf_op jit(solution)/shard_map/ppermute | solution.py:195
  54.2 1.8 %keep.1 = (bf16[8,4096]{1,0:T(8,128)(2,1)}, f32[8,4096]{1,0:T(8,128)S(1)}) custom-call(s32[2,2,32]{2,1,0:T(2,128)S(1)} %bitcast.9, s32[2,32]{1,0:T(2,128)S(1)} %bitcast.13, bf16[64,8,640]{2,1,0:T(8,128)(2,1)S(1)} %all_to_all.18.back, bf16[32,2,2,128,128]{4,3,2,1,0:T(8,128)(2,1)S(1)} %get-tuple-element.11.a_ref, bf16[8,4096]{1,0:T(8,128)(2,1)S(1)} %get-tuple-element.13.dagg_ref), custom_call_target="tpu_custom_call" | custom-call | tf_op jit(solution)/shard_map/keep/pallas_call | solution.py:140
  56.0 0.0 collective-permute-done.1.got
  56.0 0.6 %merge.1 = (bf16[8,4096]{1,0:T(8,128)(2,1)}, f32[8,512]{1,0:T(8,128)}) custom-call(f32[8,4096]{1,0:T(8,128)S(1)} %get-tuple-element.15.own, f32[8,4608]{1,0:T(8,128)S(1)} %get-tuple-element.16.sent, f32[8,4608]{1,0:T(8,128)S(1)} %collective-permute-done.1.got), custom_call_target="tpu_custom_call" | custom-call | tf_op jit(solution)/shard_map/merge/pallas_call | solution.py:140
Async XLA Ops:
  0.6 4.4 %copy-start.2 = (s32[32,2]{0,1:T(2,128)S(1)}, s32[32,2]{0,1:T(2,128)}, u32[]{:S(2)}) copy-start(s32[32,2]{0,1:T(2,128)} %param.9) | copy-start | bytes 772
  0.6 4.4 %copy-start.1 = (s32[32,2,2]{0,2,1:T(2,128)S(1)}, s32[32,2,2]{0,2,1:T(2,128)}, u32[]{:S(2)}) copy-start(s32[32,2,2]{0,2,1:T(2,128)} %param.8) | copy-start | bytes 1540
  0.7 4.4 %copy-start = (bf16[8,4096]{1,0:T(8,128)(2,1)S(1)}, bf16[8,4096]{1,0:T(8,128)(2,1)}, u32[]{:S(2)}) copy-start(bf16[8,4096]{1,0:T(8,128)(2,1)} %cot.1) | copy-start | bytes 196612
  0.7 4.4 %copy-start.3 = (bf16[8,512]{1,0:T(8,128)(2,1)S(1)}, bf16[8,512]{1,0:T(8,128)(2,1)}, u32[]{:S(2)}) copy-start(bf16[8,512]{1,0:T(8,128)(2,1)} %weight.1) | copy-start | bytes 24580
  0.7 4.3 %collective-permute-start = (bf16[8,4096]{1,0:T(8,128)(2,1)}, bf16[8,4096]{1,0:T(8,128)(2,1)S(1)}, u32[]{:S(2)}, u32[]{:S(2)}) collective-permute-start(bf16[8,4096]{1,0:T(8,128)(2,1)} %own_hbm.1), channel_id=1, source_target_pairs={{0,64},{64,0},{1,65},{65,1},{2,66},{66,2},{3,67},{67,3},{4,68},{68... | collective-permute-start | bytes 196616 | tf_op jit(solution)/shard_map/ppermute | solution.py:157
  51.2 4.8 %collective-permute-start.1 = (f32[8,4608]{1,0:T(8,128)S(1)}, f32[8,4608]{1,0:T(8,128)S(1)}, u32[]{:S(2)}, u32[]{:S(2)}) collective-permute-start(f32[8,4608]{1,0:T(8,128)S(1)} %get-tuple-element.16.sent), channel_id=1, source_target_pairs={{0,64},{64,0},{1,65},{65,1},{2,66},{66,2},{3,67},{67,3},{4,68},{68... | collective-permute-start | bytes 442376 | tf_op jit(solution)/shard_map/ppermute | solution.py:195

commit v3 on v0

v3 whole, which is shorter than its diff:
```python
import functools

import jax
import jax.numpy as jnp
from jax import lax
from jax.experimental import pallas as pl
from jax.experimental.pallas import tpu as pltpu
from jax.sharding import PartitionSpec as P

SWAP = [(0, 1), (1, 0)]
VMEM_LIMIT = 4 << 20
CHUNKS = 4
LANE = 128
ORDER_SEED = (
    29, 28, 24, 33, 35, 60, 23, 40, 11, 27, 61, 3, 5, 7, 42, 45,
    12, 59, 0, 55, 1, 44, 41, 14, 15, 17, 47, 20, 63, 10, 62, 54,
    36, 51, 21, 4, 43, 52, 9, 38, 34, 58, 39, 6, 46, 18, 8, 57,
    13, 37, 22, 30, 19, 53, 50, 25, 31, 32, 16, 2, 26, 56, 48, 49,
)


def order(ranks):
    listed = [d for d in ORDER_SEED if d < ranks]
    slots = [0] * ranks
    for slot, device in enumerate(listed):
        slots[device] = slot
    return listed, slots


def exchange(message):
    listed, _ = order(lax.axis_size("col"))
    return lax.all_to_all(message, "col", 0, 0, tiled=True, axis_index_groups=[listed])


def upper(shape):
    return lax.broadcasted_iota(jnp.int32, shape, len(shape) - 2) % 8 < 4


def swap_rows(x):
    tiles = x.reshape(x.shape[0] // 8, 8, x.shape[1])
    return pltpu.roll(tiles, 4, 1).reshape(x.shape)


def live_column(table, s, k, b):
    entry = table[s, k, b]
    return entry >= 0, pl.multiple_of(jnp.maximum(entry, 0), LANE)


def aggregate(table, feats, a_ref, s, b):
    total = jnp.zeros((8, LANE), jnp.float32)
    for k in range(2):
        live, col = live_column(table, s, k, b)
        x = feats[:, pl.ds(col, LANE)]
        x = lax.select(live, x, jnp.zeros_like(x))
        total += lax.dot_general(
            x, a_ref[b, s, k], (((1,), (1,)), ((), ())), preferred_element_type=jnp.float32
        )
    return total


def spread(table, dagg, a_ref, s, b, terms):
    for k in range(2):
        live, col = live_column(table, s, k, b)
        term = jnp.dot(dagg, a_ref[b, s, k], preferred_element_type=jnp.float32)
        term = lax.select(live, term, jnp.zeros_like(term))
        terms[:, pl.ds(col, LANE)] += term


def first_kernel(cols_hbm, counts_hbm, own_hbm, a_hbm, table, a_ref, total, own, cols, counts, sems):
    row = lax.axis_index("row")
    blocks = a_ref.shape[0]
    per = blocks // CHUNKS
    small = [
        pltpu.make_async_copy(src, dst, sems.at[i])
        for i, (src, dst) in enumerate(((cols_hbm, cols), (counts_hbm, counts), (own_hbm, own)))
    ]
    large = []
    for s in (row, 1 - row):
        for c in range(CHUNKS):
            here = pl.ds(c * per, per)
            large.append(
                pltpu.make_async_copy(
                    a_hbm.at[here, s], a_ref.at[here, s], sems.at[len(small) + len(large)]
                )
            )
    for copy in small + large:
        copy.start()
    for copy in small:
        copy.wait()
    for s in range(2):
        for b in range(blocks):
            for k in range(2):
                table[s, k, b] = jnp.where(k < counts[s, b], cols[s, k, b] * LANE, -1)
    for b in range(blocks):
        if b % per == 0:
            large[b // per].wait()
        total[:, b * LANE : (b + 1) * LANE] = aggregate(table, own, a_ref, row, b)
    for copy in large[CHUNKS:]:
        copy.wait()


def second_kernel(slots, table, other, a_ref, part, weight, cot, msg):
    row = lax.axis_index("row")
    half = weight.shape[1] // 2
    low = weight[:, :half].astype(jnp.float32)
    high = weight[:, half:].astype(jnp.float32)
    mask = upper(low.shape)
    w = (
        jnp.where(mask, low, swap_rows(high)).astype(jnp.bfloat16),
        jnp.where(mask, swap_rows(low), high).astype(jnp.bfloat16),
    )
    for b in range(a_ref.shape[0]):
        here = slice(b * LANE, (b + 1) * LANE)
        total = part[:, here] + aggregate(table, other, a_ref, 1 - row, b)
        total = total.astype(jnp.bfloat16)
        c = cot[:, here]
        c = (c, swap_rows(c.astype(jnp.float32)).astype(jnp.bfloat16))
        for q in range(2):
            slot = slots[2 * b + q]
            msg[slot, :, :LANE] = total
            msg[slot, :, LANE : 2 * LANE] = c[q]
            msg[slot, :, 2 * LANE :] = w[q]


def dense_kernel(slots, msg, back):
    half = len(slots) // 2
    tiles = [msg[8 * slot : 8 * slot + 8, :LANE].astype(jnp.float32) for slot in slots]
    agg = jnp.concatenate(
        [jnp.concatenate(tiles[:half], 0), jnp.concatenate(tiles[half:], 0)], 1
    ).astype(jnp.bfloat16)
    w = msg[:, 2 * LANE :]
    pre = jnp.dot(w, agg, preferred_element_type=jnp.float32)
    pre = pre[:, :LANE] + swap_rows(pre[:, LANE:])
    cot = msg[:, LANE : 2 * LANE].astype(jnp.float32)
    sig = jax.nn.sigmoid(pre)
    back[:, LANE : 2 * LANE] = (pre * sig).astype(jnp.bfloat16)
    dpre = cot * sig * (1.0 + pre * (1.0 - sig))
    dpre = jnp.where(upper(dpre.shape), dpre, 0.0)
    dpre = jnp.concatenate([dpre, swap_rows(dpre)], 1).astype(jnp.bfloat16)
    dagg = lax.dot_general(w, dpre, (((0,), (0,)), ((), ())), preferred_element_type=jnp.float32)
    for device, slot in enumerate(slots):
        rows = (device % half) * 8
        lanes = (device // half) * LANE
        back[8 * slot : 8 * slot + 8, :LANE] = dagg[rows : rows + 8, lanes : lanes + LANE].astype(
            jnp.bfloat16
        )
    grad = lax.dot_general(dpre, agg, (((1,), (1,)), ((), ())), preferred_element_type=jnp.float32)
    back[:, 2 * LANE :] = grad.astype(jnp.bfloat16)


def send_kernel(slots, table, back, a_ref, send, dagg_ref):
    row = lax.axis_index("row")
    blocks = a_ref.shape[0]
    slab = blocks * LANE
    half = (send.shape[1] - slab) // 2
    send[...] = jnp.zeros_like(send)
    grads = [jnp.zeros((8, half), jnp.float32) for _ in range(2)]
    for b in range(blocks):
        dagg = jnp.zeros((8, LANE), jnp.float32)
        for q in range(2):
            tile = back.at[slots[2 * b + q]]
            dagg += tile[:, :LANE].astype(jnp.float32)
            grads[q] += tile[:, 2 * LANE :].astype(jnp.float32)
        dagg = dagg.astype(jnp.bfloat16)
        dagg_ref[:, b * LANE : (b + 1) * LANE] = dagg
        spread(table, dagg, a_ref, 1 - row, b, send)
    mask = upper((8, half))
    send[:, slab : slab + half] = jnp.where(mask, grads[0], swap_rows(grads[1]))
    send[:, slab + half :] = jnp.where(mask, swap_rows(grads[0]), grads[1])


def keep_kernel(slots, table, back, a_ref, dagg_ref, out_hbm, own, out, sem):
    row = lax.axis_index("row")
    blocks = a_ref.shape[0]
    mask = upper((8, LANE))
    for b in range(blocks):
        first, second = (
            back[slots[2 * b + q], :, LANE : 2 * LANE].astype(jnp.float32) for q in range(2)
        )
        out[:, b * LANE : (b + 1) * LANE] = jnp.where(mask, first, swap_rows(second)).astype(
            jnp.bfloat16
        )
    copy = pltpu.make_async_copy(out, out_hbm, sem)
    copy.start()
    own[...] = jnp.zeros_like(own)
    for b in range(blocks):
        spread(table, dagg_ref[:, b * LANE : (b + 1) * LANE], a_ref, row, b, own)
    copy.wait()


def merge_kernel(scale, own, sent, got, grad_features, grad_weight):
    slab = own.shape[1]
    grad_features[...] = (own[...] + got[:, :slab]).astype(jnp.bfloat16)
    grad_weight[...] = (sent[:, slab:] + got[:, slab:]) * scale


HBM, VMEM, SMEM = (pl.BlockSpec(memory_space=m) for m in (pltpu.HBM, pltpu.VMEM, pltpu.SMEM))


def call(kernel, name, operands, outs, scratch=()):
    return pl.pallas_call(
        kernel,
        in_specs=[space for space, _ in operands],
        out_specs=[space for space, _, _ in outs],
        out_shape=[jax.ShapeDtypeStruct(shape, dtype) for _, shape, dtype in outs],
        scratch_shapes=list(scratch),
        compiler_params=pltpu.CompilerParams(vmem_limit_bytes=VMEM_LIMIT),
        name=name,
    )(*(array for _, array in operands))


def local(features, a_blocks, block_cols, block_counts, weight, cotangent):
    fd, slab = features.shape
    width = weight.shape[1]
    lanes = 2 * LANE + width // 2
    ranks = lax.axis_size("col")
    slots = order(ranks)[1]
    cols, counts = block_cols.transpose(1, 2, 0), block_counts.transpose(1, 0)
    bf16, f32, i32 = jnp.bfloat16, jnp.float32, jnp.int32

    other = lax.ppermute(features, "row", SWAP)
    table, blocks, part = call(
        first_kernel,
        "first",
        [
            (HBM, pltpu.with_memory_space_constraint(x, pltpu.HBM))
            for x in (cols, counts, features, a_blocks)
        ],
        [(SMEM, cols.shape, i32), (VMEM, a_blocks.shape, bf16), (VMEM, (fd, slab), f32)],
        [
            pltpu.VMEM(features.shape, bf16),
            pltpu.SMEM(cols.shape, i32),
            pltpu.SMEM(counts.shape, i32),
            pltpu.SemaphoreType.DMA((3 + 2 * CHUNKS,)),
        ],
    )
    (msg,) = call(
        functools.partial(second_kernel, slots),
        "second",
        [(SMEM, table)] + [(VMEM, x) for x in (other, blocks, part, weight, cotangent)],
        [(VMEM, (ranks, fd, lanes), bf16)],
    )
    msg = exchange(msg.reshape(ranks * fd, lanes))
    (back,) = call(
        functools.partial(dense_kernel, slots), "dense", [(VMEM, msg)], [(VMEM, msg.shape, bf16)]
    )
    back = exchange(back).reshape(ranks, fd, lanes)
    send, dagg = call(
        functools.partial(send_kernel, slots),
        "send",
        [(SMEM, table), (VMEM, back), (VMEM, blocks)],
        [(VMEM, (fd, slab + width), f32), (VMEM, (fd, slab), bf16)],
    )
    got = lax.ppermute(send, "row", SWAP)
    output, own = call(
        functools.partial(keep_kernel, slots),
        "keep",
        [(SMEM, table), (VMEM, back), (VMEM, blocks), (VMEM, dagg)],
        [(HBM, (fd, slab), bf16), (VMEM, (fd, slab), f32)],
        [pltpu.VMEM((fd, slab), bf16), pltpu.SemaphoreType.DMA],
    )
    scale = 1.0 / (slab * lax.axis_size("row")) ** 0.5
    grad_features, grad_weight = call(
        functools.partial(merge_kernel, scale),
        "merge",
        [(VMEM, own), (VMEM, send), (VMEM, got)],
        [(VMEM, (fd, slab), bf16), (VMEM, (fd, width), f32)],
    )
    return output, grad_weight, grad_features


def solution(mesh):
    placed = (
        P("col", "row"),
        P("row", None, None, None, None),
        P("row", None, None),
        P("row", None),
        P("col", None),
        P("col", "row"),
    )
    return jax.shard_map(
        local,
        mesh=mesh,
        in_specs=placed,
        out_specs=(P("col", "row"), P("col", None), P("col", "row")),
        check_vma=False,
    )
```

time: 528 us -> 51.2 us (0.10)
  waiting for transfers between devices: 415 us -> 0.01 us
  matrix products: 19.4 us -> 0 us
  local copies, waits for them, and re-layouts: 15.3 us -> 0.01 us
  other arithmetic: 14.6 us -> 0 us
  between operations: 13.8 us -> 0.71 us
  blocking collectives: 48.7 us -> 36.2 us
  Pallas kernels: 0 us -> 9.37 us
    unnamed x5 -> x0, waiting for transfers between devices: 323 us -> none
    all_gather x1 -> x0, waiting for transfers between devices: 68.5 us -> none  [local(): agg_full = lax.all_gather(aggregated, 'col', axis=0, tiled=True)]
    psum x1 -> x0, blocking collectives: 48.7 us -> none  [local(): lax.psum(local_grad, 'row') / jnp.sqrt(jnp.float32(node_total))]
    all_to_all x0 -> x2, blocking collectives: none -> 36.2 us  [exchange(): lax.all_to_all(message, 'col', 0, 0, tiled=True, axis_index_groups=[listed])]
    psum x1 -> x0, waiting for transfers between devices: 23 us -> none  [from_root(): return lax.psum(kept, axis)]
    dot_general x6 -> x0, matrix products: 19.4 us -> none  [the longest x2 5.14 us: local(): jnp.einsum('fbkj,bkij->fbi', picked, masked[:, section_idx], preferred_el...]
    unnamed x10 -> x4, local copies, waits for them, and re-layouts: 11.7 us -> 0.01 us
    pallas_call x0 -> x6, Pallas kernels: none -> 9.37 us  [call(): pl.pallas_call(kernel, in_specs=[space for space, _ in operands], out_spe...]
  transfers between devices with their start and end apart: 4 -> 2, of which waited for: 3 -> 0; matrix products, arithmetic and copies ran while one was open for 2% -> 0% of each run, Pallas kernels for 0% -> 10%
where the time goes in v3:
time: 51.2 us; the launch traced here: 51 us
  blocking collectives  36.2 us (71%)
  Pallas kernels  9.37 us (18%)
  starting transfers between devices  4.76 us (9%)
  between operations  0.71 us (1%)
    all_to_all x2, blocking collectives, exchange(): lax.all_to_all(message, 'col', 0, 0, tiled=True, axis_index_groups=[listed])  36.2 us
    pallas_call x6, Pallas kernels, call(): pl.pallas_call(kernel, in_specs=[space for space, _ in operands], out_spe...  9.37 us
    ppermute x1, starting transfers between devices, local(): got = lax.ppermute(send, 'row', SWAP)  3.3 us
    ppermute x1, starting transfers between devices, local(): other = lax.ppermute(features, 'row', SWAP)  1.46 us
  transfers between devices with their start and end apart: 2, of which 0 were waited for; matrix products, arithmetic and copies ran while one was open for 0% of the time, Pallas kernels for 10%

profile of v3, /device:TPU:1, one launch (start us, length us, event | category | flops | bytes accessed | tf_op | source)
XLA Modules:
  0.0 51.0 jit_solution(14111610095291767597)
XLA Ops:
  0.6 0.0 copy-start
  0.6 0.0 copy-start.1
  0.7 1.5 %collective-permute-start = (bf16[8,4096]{1,0:T(8,128)(2,1)}, bf16[8,4096]{1,0:T(8,128)(2,1)S(1)}, u32[]{:S(2)}, u32[]{:S(2)}) collective-permute-start(bf16[8,4096]{1,0:T(8,128)(2,1)} %own_hbm.1), channel_id=1, source_target_pairs={{0,64},{64,0},{1,65},{65,1},{2,66},{66,2},{3,67},{67,3},{4,68},{68... | collective-permute-start | bytes 196616 | tf_op jit(solution)/shard_map/ppermute | solution.py:221
  2.1 3.4 %first.1 = (s32[2,2,32]{2,1,0:T(2,128)S(1)}, bf16[32,2,2,128,128]{4,3,2,1,0:T(8,128)(2,1)S(1)}, f32[8,4096]{1,0:T(8,128)S(1)}) custom-call(s32[2,2,32]{2,1,0:T(2,128)} %bitcast.6, s32[2,32]{1,0:T(2,128)} %bitcast.7, bf16[8,4096]{1,0:T(8,128)(2,1)} %own_hbm.1, bf16[32,2,2,128,128]{4,3,2,1,0:T(8,128)(2,1)} %a_hbm.1), custom_call_target="tpu_custom_call" | custom-call | tf_op jit(solution)/shard_map/first/pallas_call | solution.py:201
  5.5 0.0 collective-permute-done.other
  5.5 0.0 copy-done
  5.5 0.0 copy-done.1
  5.5 1.8 %second.1 = bf16[64,8,512]{2,1,0:T(8,128)(2,1)S(1)} custom-call(s32[2,2,32]{2,1,0:T(2,128)S(1)} %get-tuple-element.12.table, bf16[8,4096]{1,0:T(8,128)(2,1)S(1)} %collective-permute-done.other, bf16[32,2,2,128,128]{4,3,2,1,0:T(8,128)(2,1)S(1)} %get-tuple-element.13.a_ref, f32[8,4096]{1,0:T(8,128)S(1)} %get-tuple-element.14.part, ...), custom_call_target="tpu_custom_call" | custom-call | tf_op jit(solution)/shard_map/second/pallas_call | solution.py:201
  7.3 20.5 %all_to_all.17 = bf16[64,8,512]{2,1,0:T(8,128)(2,1)S(1)} all-to-all(bf16[64,8,512]{2,1,0:T(8,128)(2,1)S(1)} %second.1), channel_id=1, replica_groups={{29,28,24,33,35,60,23,40,11,27,61,3,5,7,42,45,12,59,0,55,1,44,41,14,15,..., dimensions={0} | all-to-all | bytes 1048576 | tf_op jit(solution)/shard_map/all_to_all | solution.py:32
  27.8 0.5 %dense.1 = bf16[512,512]{1,0:T(8,128)(2,1)S(1)} custom-call(bf16[512,512]{1,0:T(8,128)(2,1)S(1)} %bitcast.4), custom_call_target="tpu_custom_call" | custom-call | tf_op jit(solution)/shard_map/dense/pallas_call | solution.py:201
  28.3 15.7 %all_to_all.18.back = bf16[64,8,512]{2,1,0:T(8,128)(2,1)S(1)} all-to-all(bf16[64,8,512]{2,1,0:T(8,128)(2,1)S(1)} %bitcast.5), channel_id=1, replica_groups={{29,28,24,33,35,60,23,40,11,27,61,3,5,7,42,45,12,59,0,55,1,44,41,14,15,..., dimensions={0} | all-to-all | bytes 1048576 | tf_op jit(solution)/shard_map/all_to_all | solution.py:32
  44.0 1.3 %send.1 = (f32[8,4608]{1,0:T(8,128)S(1)}, bf16[8,4096]{1,0:T(8,128)(2,1)S(1)}) custom-call(s32[2,2,32]{2,1,0:T(2,128)S(1)} %get-tuple-element.12.table, bf16[64,8,512]{2,1,0:T(8,128)(2,1)S(1)} %all_to_all.18.back, bf16[32,2,2,128,128]{4,3,2,1,0:T(8,128)(2,1)S(1)} %get-tuple-element.13.a_ref), custom_call_target="tpu_custom_call" | custom-call | tf_op jit(solution)/shard_map/send/pallas_call | solution.py:201
  45.2 3.3 %collective-permute-start.1 = (f32[8,4608]{1,0:T(8,128)S(1)}, f32[8,4608]{1,0:T(8,128)S(1)}, u32[]{:S(2)}, u32[]{:S(2)}) collective-permute-start(f32[8,4608]{1,0:T(8,128)S(1)} %get-tuple-element.18.sent), channel_id=1, source_target_pairs={{0,64},{64,0},{1,65},{65,1},{2,66},{66,2},{3,67},{67,3},{4,68},{68... | collective-permute-start | bytes 442376 | tf_op jit(solution)/shard_map/ppermute | solution.py:254
  48.5 1.8 %keep.1 = (bf16[8,4096]{1,0:T(8,128)(2,1)}, f32[8,4096]{1,0:T(8,128)S(1)}) custom-call(s32[2,2,32]{2,1,0:T(2,128)S(1)} %get-tuple-element.12.table, bf16[64,8,512]{2,1,0:T(8,128)(2,1)S(1)} %all_to_all.18.back, bf16[32,2,2,128,128]{4,3,2,1,0:T(8,128)(2,1)S(1)} %get-tuple-element.13.a_ref, bf16[8,4096]{1,0:T(8,128)(2,1)S(1)} %get-tuple-element.15.dagg_ref), custom_call_target="tpu_custom_call" | custom-call | tf_op jit(solution)/shard_map/keep/pallas_call | solution.py:201
  50.4 0.0 collective-permute-done.1.got
  50.4 0.6 %merge.1 = (bf16[8,4096]{1,0:T(8,128)(2,1)}, f32[8,512]{1,0:T(8,128)}) custom-call(f32[8,4096]{1,0:T(8,128)S(1)} %get-tuple-element.17.own, f32[8,4608]{1,0:T(8,128)S(1)} %get-tuple-element.18.sent, f32[8,4608]{1,0:T(8,128)S(1)} %collective-permute-done.1.got), custom_call_target="tpu_custom_call" | custom-call | tf_op jit(solution)/shard_map/merge/pallas_call | solution.py:201
Async XLA Ops:
  0.6 4.9 %copy-start = (bf16[8,4096]{1,0:T(8,128)(2,1)S(1)}, bf16[8,4096]{1,0:T(8,128)(2,1)}, u32[]{:S(2)}) copy-start(bf16[8,4096]{1,0:T(8,128)(2,1)} %cot.1) | copy-start | bytes 196612
  0.6 4.9 %copy-start.1 = (bf16[8,512]{1,0:T(8,128)(2,1)S(1)}, bf16[8,512]{1,0:T(8,128)(2,1)}, u32[]{:S(2)}) copy-start(bf16[8,512]{1,0:T(8,128)(2,1)} %weight.1) | copy-start | bytes 24580
  0.7 4.8 %collective-permute-start = (bf16[8,4096]{1,0:T(8,128)(2,1)}, bf16[8,4096]{1,0:T(8,128)(2,1)S(1)}, u32[]{:S(2)}, u32[]{:S(2)}) collective-permute-start(bf16[8,4096]{1,0:T(8,128)(2,1)} %own_hbm.1), channel_id=1, source_target_pairs={{0,64},{64,0},{1,65},{65,1},{2,66},{66,2},{3,67},{67,3},{4,68},{68... | collective-permute-start | bytes 196616 | tf_op jit(solution)/shard_map/ppermute | solution.py:221
  45.2 5.1 %collective-permute-start.1 = (f32[8,4608]{1,0:T(8,128)S(1)}, f32[8,4608]{1,0:T(8,128)S(1)}, u32[]{:S(2)}, u32[]{:S(2)}) collective-permute-start(f32[8,4608]{1,0:T(8,128)S(1)} %get-tuple-element.18.sent), channel_id=1, source_target_pairs={{0,64},{64,0},{1,65},{65,1},{2,66},{66,2},{3,67},{67,3},{4,68},{68... | collective-permute-start | bytes 442376 | tf_op jit(solution)/shard_map/ppermute | solution.py:254

commit v4 on v3

--- a/solution.py
+++ b/solution.py
@@ -41,38 +41,41 @@
     return pltpu.roll(tiles, 4, 1).reshape(x.shape)
 
 
-def live_column(table, s, k, b):
-    entry = table[s, k, b]
-    return entry >= 0, pl.multiple_of(jnp.maximum(entry, 0), LANE)
-
-
 def aggregate(table, feats, a_ref, s, b):
-    total = jnp.zeros((8, LANE), jnp.float32)
+    return lax.dot_general(
+        jnp.concatenate([feats[:, column(table, s, k, b)] for k in range(2)], 1),
+        jnp.concatenate([a_ref[b, s, k] for k in range(2)], 1),
+        (((1,), (1,)), ((), ())),
+        preferred_element_type=jnp.float32,
+    )
+
+
+def spread(table, dagg, a_ref, s, b, terms):
+    both = jnp.dot(
+        dagg,
+        jnp.concatenate([a_ref[b, s, k] for k in range(2)], 1),
+        preferred_element_type=jnp.float32,
+    )
     for k in range(2):
-        live, col = live_column(table, s, k, b)
-        x = feats[:, pl.ds(col, LANE)]
-        x = lax.select(live, x, jnp.zeros_like(x))
-        total += lax.dot_general(
-            x, a_ref[b, s, k], (((1,), (1,)), ((), ())), preferred_element_type=jnp.float32
-        )
-    return total
-
-
-def spread(table, dagg, a_ref, s, b, terms):
-    for k in range(2):
-        live, col = live_column(table, s, k, b)
-        term = jnp.dot(dagg, a_ref[b, s, k], preferred_element_type=jnp.float32)
-        term = lax.select(live, term, jnp.zeros_like(term))
-        terms[:, pl.ds(col, LANE)] += term
-
-
-def first_kernel(cols_hbm, counts_hbm, own_hbm, a_hbm, table, a_ref, total, own, cols, counts, sems):
+        terms[:, column(table, s, k, b)] += both[:, k * LANE : (k + 1) * LANE]
+
+
+def column(table, s, k, b):
+    return pl.ds(pl.multiple_of(table[s, k, b], LANE), LANE)
+
+
+def first_kernel(
+    cols_hbm, counts_hbm, own_hbm, a_hbm, table, a_ref, total, own, cols, counts, scalars, sems
+):
     row = lax.axis_index("row")
     blocks = a_ref.shape[0]
+    slab = total.shape[1]
     per = blocks // CHUNKS
     small = [
         pltpu.make_async_copy(src, dst, sems.at[i])
-        for i, (src, dst) in enumerate(((cols_hbm, cols), (counts_hbm, counts), (own_hbm, own)))
+        for i, (src, dst) in enumerate(
+            ((cols_hbm, cols), (counts_hbm, counts), (own_hbm, own.at[:, pl.ds(0, slab)]))
+        )
     ]
     large = []
     for s in (row, 1 - row):
@@ -85,22 +88,29 @@
             )
     for copy in small + large:
         copy.start()
-    for copy in small:
-        copy.wait()
+    own[:, slab:] = jnp.zeros((8, LANE), own.dtype)
+    small[0].wait()
+    small[1].wait()
     for s in range(2):
-        for b in range(blocks):
-            for k in range(2):
-                table[s, k, b] = jnp.where(k < counts[s, b], cols[s, k, b] * LANE, -1)
+        live = lax.broadcasted_iota(jnp.int32, cols.shape[1:], 0) < counts[s : s + 1]
+        table[s] = jnp.where(live, cols[s] * LANE, slab)
+    listed = pltpu.make_async_copy(table, scalars, sems.at[0])
+    listed.start()
+    listed.wait()
+    small[2].wait()
     for b in range(blocks):
         if b % per == 0:
             large[b // per].wait()
-        total[:, b * LANE : (b + 1) * LANE] = aggregate(table, own, a_ref, row, b)
+        total[:, b * LANE : (b + 1) * LANE] = aggregate(scalars, own, a_ref, row, b)
     for copy in large[CHUNKS:]:
         copy.wait()
 
 
-def second_kernel(slots, table, other, a_ref, part, weight, cot, msg):
-    row = lax.axis_index("row")
+def second_kernel(slots, table, other, a_ref, part, weight, cot, msg, feats):
+    row = lax.axis_index("row")
+    slab = other.shape[1]
+    feats[:, :slab] = other[...]
+    feats[:, slab:] = jnp.zeros((8, LANE), feats.dtype)
     half = weight.shape[1] // 2
     low = weight[:, :half].astype(jnp.float32)
     high = weight[:, half:].astype(jnp.float32)
@@ -111,7 +121,7 @@
     )
     for b in range(a_ref.shape[0]):
         here = slice(b * LANE, (b + 1) * LANE)
-        total = part[:, here] + aggregate(table, other, a_ref, 1 - row, b)
+        total = part[:, here] + aggregate(table, feats, a_ref, 1 - row, b)
         total = total.astype(jnp.bfloat16)
         c = cot[:, here]
         c = (c, swap_rows(c.astype(jnp.float32)).astype(jnp.bfloat16))
@@ -189,8 +199,8 @@
 
 
 def merge_kernel(scale, own, sent, got, grad_features, grad_weight):
-    slab = own.shape[1]
-    grad_features[...] = (own[...] + got[:, :slab]).astype(jnp.bfloat16)
+    slab = grad_features.shape[1]
+    grad_features[...] = (own[:, :slab] + got[:, :slab]).astype(jnp.bfloat16)
     grad_weight[...] = (sent[:, slab:] + got[:, slab:]) * scale
 
 
@@ -226,11 +236,12 @@
             (HBM, pltpu.with_memory_space_constraint(x, pltpu.HBM))
             for x in (cols, counts, features, a_blocks)
         ],
-        [(SMEM, cols.shape, i32), (VMEM, a_blocks.shape, bf16), (VMEM, (fd, slab), f32)],
+        [(VMEM, cols.shape, i32), (VMEM, a_blocks.shape, bf16), (VMEM, (fd, slab), f32)],
         [
-            pltpu.VMEM(features.shape, bf16),
+            pltpu.VMEM((fd, slab + LANE), bf16),
+            pltpu.VMEM(cols.shape, i32),
+            pltpu.VMEM(counts.shape, i32),
             pltpu.SMEM(cols.shape, i32),
-            pltpu.SMEM(counts.shape, i32),
             pltpu.SemaphoreType.DMA((3 + 2 * CHUNKS,)),
         ],
     )
@@ -239,6 +250,7 @@
         "second",
         [(SMEM, table)] + [(VMEM, x) for x in (other, blocks, part, weight, cotangent)],
         [(VMEM, (ranks, fd, lanes), bf16)],
+        [pltpu.VMEM((fd, slab + LANE), bf16)],
     )
     msg = exchange(msg.reshape(ranks * fd, lanes))
     (back,) = call(
@@ -256,7 +268,7 @@
         functools.partial(keep_kernel, slots),
         "keep",
         [(SMEM, table), (VMEM, back), (VMEM, blocks), (VMEM, dagg)],
-        [(HBM, (fd, slab), bf16), (VMEM, (fd, slab), f32)],
+        [(HBM, (fd, slab), bf16), (VMEM, (fd, slab + LANE), f32)],
         [pltpu.VMEM((fd, slab), bf16), pltpu.SemaphoreType.DMA],
     )
     scale = 1.0 / (slab * lax.axis_size("row")) ** 0.5

time: 51.2 us -> 49.3 us (0.963)
  Pallas kernels: 9.37 us -> 7.46 us
    pallas_call x6, Pallas kernels: 9.37 us -> 7.46 us  [call(): pl.pallas_call(kernel, in_specs=[space for space, _ in operands], out_spe...]
  transfers between devices with their start and end apart: 2 -> 2, of which waited for: 0 -> 0; matrix products, arithmetic and copies ran while one was open for 0% -> 0% of each run, Pallas kernels for 10% -> 8%
where the time goes in v4:
time: 49.3 us; the launch traced here: 49.1 us
  blocking collectives  36.2 us (73%)
  Pallas kernels  7.46 us (15%)
  starting transfers between devices  4.78 us (10%)
  between operations  0.71 us (1%)
    all_to_all x2, blocking collectives, exchange(): lax.all_to_all(message, 'col', 0, 0, tiled=True, axis_index_groups=[listed])  36.2 us
    pallas_call x6, Pallas kernels, call(): pl.pallas_call(kernel, in_specs=[space for space, _ in operands], out_spe...  7.46 us
    ppermute x1, starting transfers between devices, local(): got = lax.ppermute(send, 'row', SWAP)  3.32 us
    ppermute x1, starting transfers between devices, local(): other = lax.ppermute(features, 'row', SWAP)  1.46 us
  transfers between devices with their start and end apart: 2, of which 0 were waited for; matrix products, arithmetic and copies ran while one was open for 0% of the time, Pallas kernels for 8%

profile of v4, /device:TPU:1, one launch (start us, length us, event | category | flops | bytes accessed | tf_op | source)
XLA Modules:
  0.0 49.1 jit_solution(399073159275163112)
XLA Ops:
  0.6 0.0 copy-start
  0.6 0.0 copy-start.1
  0.7 1.5 %collective-permute-start = (bf16[8,4096]{1,0:T(8,128)(2,1)}, bf16[8,4096]{1,0:T(8,128)(2,1)S(1)}, u32[]{:S(2)}, u32[]{:S(2)}) collective-permute-start(bf16[8,4096]{1,0:T(8,128)(2,1)} %own_hbm.1), channel_id=1, source_target_pairs={{0,64},{64,0},{1,65},{65,1},{2,66},{66,2},{3,67},{67,3},{4,68},{68... | collective-permute-start | bytes 196616 | tf_op jit(solution)/shard_map/ppermute | solution.py:231
  2.1 2.4 %first.1 = (s32[2,2,32]{2,1,0:T(2,128)S(1)}, bf16[32,2,2,128,128]{4,3,2,1,0:T(8,128)(2,1)S(1)}, f32[8,4096]{1,0:T(8,128)S(1)}) custom-call(s32[2,2,32]{2,1,0:T(2,128)} %bitcast.6, s32[2,32]{1,0:T(2,128)} %bitcast.7, bf16[8,4096]{1,0:T(8,128)(2,1)} %own_hbm.1, bf16[32,2,2,128,128]{4,3,2,1,0:T(8,128)(2,1)} %a_hbm.1), custom_call_target="tpu_custom_call" | custom-call | tf_op jit(solution)/shard_map/first/pallas_call | solution.py:211
  4.5 0.0 collective-permute-done.other
  4.5 0.0 copy-done
  4.5 0.0 copy-done.1
  4.5 1.2 %second.1 = bf16[64,8,512]{2,1,0:T(8,128)(2,1)S(1)} custom-call(s32[2,2,32]{2,1,0:T(2,128)S(1)} %get-tuple-element.12.table, bf16[8,4096]{1,0:T(8,128)(2,1)S(1)} %collective-permute-done.other, bf16[32,2,2,128,128]{4,3,2,1,0:T(8,128)(2,1)S(1)} %get-tuple-element.13.a_ref, f32[8,4096]{1,0:T(8,128)S(1)} %get-tuple-element.14.part, ...), custom_call_target="tpu_custom_call" | custom-call | tf_op jit(solution)/shard_map/second/pallas_call | solution.py:211
  5.8 20.5 %all_to_all.17 = bf16[64,8,512]{2,1,0:T(8,128)(2,1)S(1)} all-to-all(bf16[64,8,512]{2,1,0:T(8,128)(2,1)S(1)} %second.1), channel_id=1, replica_groups={{29,28,24,33,35,60,23,40,11,27,61,3,5,7,42,45,12,59,0,55,1,44,41,14,15,..., dimensions={0} | all-to-all | bytes 1048576 | tf_op jit(solution)/shard_map/all_to_all | solution.py:32
  26.3 0.5 %dense.1 = bf16[512,512]{1,0:T(8,128)(2,1)S(1)} custom-call(bf16[512,512]{1,0:T(8,128)(2,1)S(1)} %bitcast.4), custom_call_target="tpu_custom_call" | custom-call | tf_op jit(solution)/shard_map/dense/pallas_call | solution.py:211
  26.8 15.7 %all_to_all.18.back = bf16[64,8,512]{2,1,0:T(8,128)(2,1)S(1)} all-to-all(bf16[64,8,512]{2,1,0:T(8,128)(2,1)S(1)} %bitcast.5), channel_id=1, replica_groups={{29,28,24,33,35,60,23,40,11,27,61,3,5,7,42,45,12,59,0,55,1,44,41,14,15,..., dimensions={0} | all-to-all | bytes 1048576 | tf_op jit(solution)/shard_map/all_to_all | solution.py:32
  42.5 1.0 %send.1 = (f32[8,4608]{1,0:T(8,128)S(1)}, bf16[8,4096]{1,0:T(8,128)(2,1)S(1)}) custom-call(s32[2,2,32]{2,1,0:T(2,128)S(1)} %get-tuple-element.12.table, bf16[64,8,512]{2,1,0:T(8,128)(2,1)S(1)} %all_to_all.18.back, bf16[32,2,2,128,128]{4,3,2,1,0:T(8,128)(2,1)S(1)} %get-tuple-element.13.a_ref), custom_call_target="tpu_custom_call" | custom-call | tf_op jit(solution)/shard_map/send/pallas_call | solution.py:211
  43.5 3.3 %collective-permute-start.1 = (f32[8,4608]{1,0:T(8,128)S(1)}, f32[8,4608]{1,0:T(8,128)S(1)}, u32[]{:S(2)}, u32[]{:S(2)}) collective-permute-start(f32[8,4608]{1,0:T(8,128)S(1)} %get-tuple-element.18.sent), channel_id=1, source_target_pairs={{0,64},{64,0},{1,65},{65,1},{2,66},{66,2},{3,67},{67,3},{4,68},{68... | collective-permute-start | bytes 442376 | tf_op jit(solution)/shard_map/ppermute | solution.py:266
  46.8 1.6 %keep.1 = (bf16[8,4096]{1,0:T(8,128)(2,1)}, f32[8,4224]{1,0:T(8,128)S(1)}) custom-call(s32[2,2,32]{2,1,0:T(2,128)S(1)} %get-tuple-element.12.table, bf16[64,8,512]{2,1,0:T(8,128)(2,1)S(1)} %all_to_all.18.back, bf16[32,2,2,128,128]{4,3,2,1,0:T(8,128)(2,1)S(1)} %get-tuple-element.13.a_ref, bf16[8,4096]{1,0:T(8,128)(2,1)S(1)} %get-tuple-element.15.dagg_ref), custom_call_target="tpu_custom_call" | custom-call | tf_op jit(solution)/shard_map/keep/pallas_call | solution.py:211
  48.5 0.0 collective-permute-done.1.got
  48.5 0.6 %merge.1 = (bf16[8,4096]{1,0:T(8,128)(2,1)}, f32[8,512]{1,0:T(8,128)}) custom-call(f32[8,4224]{1,0:T(8,128)S(1)} %get-tuple-element.17.own, f32[8,4608]{1,0:T(8,128)S(1)} %get-tuple-element.18.sent, f32[8,4608]{1,0:T(8,128)S(1)} %collective-permute-done.1.got), custom_call_target="tpu_custom_call" | custom-call | tf_op jit(solution)/shard_map/merge/pallas_call | solution.py:211
Async XLA Ops:
  0.6 3.9 %copy-start = (bf16[8,4096]{1,0:T(8,128)(2,1)S(1)}, bf16[8,4096]{1,0:T(8,128)(2,1)}, u32[]{:S(2)}) copy-start(bf16[8,4096]{1,0:T(8,128)(2,1)} %cot.1) | copy-start | bytes 196612
  0.6 3.9 %copy-start.1 = (bf16[8,512]{1,0:T(8,128)(2,1)S(1)}, bf16[8,512]{1,0:T(8,128)(2,1)}, u32[]{:S(2)}) copy-start(bf16[8,512]{1,0:T(8,128)(2,1)} %weight.1) | copy-start | bytes 24580
  0.7 3.9 %collective-permute-start = (bf16[8,4096]{1,0:T(8,128)(2,1)}, bf16[8,4096]{1,0:T(8,128)(2,1)S(1)}, u32[]{:S(2)}, u32[]{:S(2)}) collective-permute-start(bf16[8,4096]{1,0:T(8,128)(2,1)} %own_hbm.1), channel_id=1, source_target_pairs={{0,64},{64,0},{1,65},{65,1},{2,66},{66,2},{3,67},{67,3},{4,68},{68... | collective-permute-start | bytes 196616 | tf_op jit(solution)/shard_map/ppermute | solution.py:231
  43.5 5.0 %collective-permute-start.1 = (f32[8,4608]{1,0:T(8,128)S(1)}, f32[8,4608]{1,0:T(8,128)S(1)}, u32[]{:S(2)}, u32[]{:S(2)}) collective-permute-start(f32[8,4608]{1,0:T(8,128)S(1)} %get-tuple-element.18.sent), channel_id=1, source_target_pairs={{0,64},{64,0},{1,65},{65,1},{2,66},{66,2},{3,67},{67,3},{4,68},{68... | collective-permute-start | bytes 442376 | tf_op jit(solution)/shard_map/ppermute | solution.py:266

commit v5 on v4

--- a/solution.py
+++ b/solution.py
@@ -41,9 +41,9 @@
     return pltpu.roll(tiles, 4, 1).reshape(x.shape)
 
 
-def aggregate(table, feats, a_ref, s, b):
+def aggregate(picked, a_ref, s, b):
     return lax.dot_general(
-        jnp.concatenate([feats[:, column(table, s, k, b)] for k in range(2)], 1),
+        jnp.concatenate(picked, 1),
         jnp.concatenate([a_ref[b, s, k] for k in range(2)], 1),
         (((1,), (1,)), ((), ())),
         preferred_element_type=jnp.float32,
@@ -61,11 +61,11 @@
 
 
 def column(table, s, k, b):
-    return pl.ds(pl.multiple_of(table[s, k, b], LANE), LANE)
+    return pl.ds(pl.multiple_of(table[s, k * (table.shape[1] // 2) + b, 0], LANE), LANE)
 
 
 def first_kernel(
-    cols_hbm, counts_hbm, own_hbm, a_hbm, table, a_ref, total, own, cols, counts, scalars, sems
+    cols_hbm, counts_hbm, own_hbm, a_hbm, columns, a_ref, total, own, cols, counts, table, scalars, sems
 ):
     row = lax.axis_index("row")
     blocks = a_ref.shape[0]
@@ -101,7 +101,14 @@
     for b in range(blocks):
         if b % per == 0:
             large[b // per].wait()
-        total[:, b * LANE : (b + 1) * LANE] = aggregate(scalars, own, a_ref, row, b)
+        picked = [
+            own[:, pl.ds(pl.multiple_of(scalars[row, k, b], LANE), LANE)] for k in range(2)
+        ]
+        total[:, b * LANE : (b + 1) * LANE] = aggregate(picked, a_ref, row, b)
+    for s in range(2):
+        for k in range(2):
+            for b in range(blocks):
+                columns[s, k * blocks + b, :] = jnp.full((LANE,), scalars[s, k, b], jnp.int32)
     for copy in large[CHUNKS:]:
         copy.wait()
 
@@ -121,7 +128,8 @@
     )
     for b in range(a_ref.shape[0]):
         here = slice(b * LANE, (b + 1) * LANE)
-        total = part[:, here] + aggregate(table, feats, a_ref, 1 - row, b)
+        picked = [feats[:, column(table, 1 - row, k, b)] for k in range(2)]
+        total = part[:, here] + aggregate(picked, a_ref, 1 - row, b)
         total = total.astype(jnp.bfloat16)
         c = cot[:, here]
         c = (c, swap_rows(c.astype(jnp.float32)).astype(jnp.bfloat16))
@@ -179,32 +187,29 @@
     send[:, slab + half :] = jnp.where(mask, swap_rows(grads[0]), grads[1])
 
 
-def keep_kernel(slots, table, back, a_ref, dagg_ref, out_hbm, own, out, sem):
+def keep_kernel(table, a_ref, dagg_ref, own):
     row = lax.axis_index("row")
     blocks = a_ref.shape[0]
+    own[...] = jnp.zeros_like(own)
+    for b in range(blocks):
+        spread(table, dagg_ref[:, b * LANE : (b + 1) * LANE], a_ref, row, b, own)
+
+
+def merge_kernel(slots, scale, back, own, sent, got, out, grad_features, grad_weight):
     mask = upper((8, LANE))
-    for b in range(blocks):
+    for b in range(len(slots) // 2):
         first, second = (
             back[slots[2 * b + q], :, LANE : 2 * LANE].astype(jnp.float32) for q in range(2)
         )
         out[:, b * LANE : (b + 1) * LANE] = jnp.where(mask, first, swap_rows(second)).astype(
             jnp.bfloat16
         )
-    copy = pltpu.make_async_copy(out, out_hbm, sem)
-    copy.start()
-    own[...] = jnp.zeros_like(own)
-    for b in range(blocks):
-        spread(table, dagg_ref[:, b * LANE : (b + 1) * LANE], a_ref, row, b, own)
-    copy.wait()
-
-
-def merge_kernel(scale, own, sent, got, grad_features, grad_weight):
     slab = grad_features.shape[1]
     grad_features[...] = (own[:, :slab] + got[:, :slab]).astype(jnp.bfloat16)
     grad_weight[...] = (sent[:, slab:] + got[:, slab:]) * scale
 
 
-HBM, VMEM, SMEM = (pl.BlockSpec(memory_space=m) for m in (pltpu.HBM, pltpu.VMEM, pltpu.SMEM))
+HBM, VMEM = (pl.BlockSpec(memory_space=m) for m in (pltpu.HBM, pltpu.VMEM))
 
 
 def call(kernel, name, operands, outs, scratch=()):
@@ -236,11 +241,16 @@
             (HBM, pltpu.with_memory_space_constraint(x, pltpu.HBM))
             for x in (cols, counts, features, a_blocks)
         ],
-        [(VMEM, cols.shape, i32), (VMEM, a_blocks.shape, bf16), (VMEM, (fd, slab), f32)],
+        [
+            (VMEM, (2, 2 * cols.shape[2], LANE), i32),
+            (VMEM, a_blocks.shape, bf16),
+            (VMEM, (fd, slab), f32),
+        ],
         [
             pltpu.VMEM((fd, slab + LANE), bf16),
             pltpu.VMEM(cols.shape, i32),
             pltpu.VMEM(counts.shape, i32),
+            pltpu.VMEM(cols.shape, i32),
             pltpu.SMEM(cols.shape, i32),
             pltpu.SemaphoreType.DMA((3 + 2 * CHUNKS,)),
         ],
@@ -248,7 +258,7 @@
     (msg,) = call(
         functools.partial(second_kernel, slots),
         "second",
-        [(SMEM, table)] + [(VMEM, x) for x in (other, blocks, part, weight, cotangent)],
+        [(VMEM, table)] + [(VMEM, x) for x in (other, blocks, part, weight, cotangent)],
         [(VMEM, (ranks, fd, lanes), bf16)],
         [pltpu.VMEM((fd, slab + LANE), bf16)],
     )
@@ -260,23 +270,22 @@
     send, dagg = call(
         functools.partial(send_kernel, slots),
         "send",
-        [(SMEM, table), (VMEM, back), (VMEM, blocks)],
+        [(VMEM, table), (VMEM, back), (VMEM, blocks)],
         [(VMEM, (fd, slab + width), f32), (VMEM, (fd, slab), bf16)],
     )
     got = lax.ppermute(send, "row", SWAP)
-    output, own = call(
-        functools.partial(keep_kernel, slots),
+    (own,) = call(
+        keep_kernel,
         "keep",
-        [(SMEM, table), (VMEM, back), (VMEM, blocks), (VMEM, dagg)],
-        [(HBM, (fd, slab), bf16), (VMEM, (fd, slab + LANE), f32)],
-        [pltpu.VMEM((fd, slab), bf16), pltpu.SemaphoreType.DMA],
+        [(VMEM, table), (VMEM, blocks), (VMEM, dagg)],
+        [(VMEM, (fd, slab + LANE), f32)],
     )
     scale = 1.0 / (slab * lax.axis_size("row")) ** 0.5
-    grad_features, grad_weight = call(
-        functools.partial(merge_kernel, scale),
+    output, grad_features, grad_weight = call(
+        functools.partial(merge_kernel, slots, scale),
         "merge",
-        [(VMEM, own), (VMEM, send), (VMEM, got)],
-        [(VMEM, (fd, slab), bf16), (VMEM, (fd, width), f32)],
+        [(VMEM, back), (VMEM, own), (VMEM, send), (VMEM, got)],
+        [(VMEM, (fd, slab), bf16), (VMEM, (fd, slab), bf16), (VMEM, (fd, width), f32)],
     )
     return output, grad_weight, grad_features
 

time: 49.3 us -> 47.6 us (0.966)
  Pallas kernels: 7.46 us -> 5.26 us
  waiting for transfers between devices: 0.01 us -> 0.52 us
    pallas_call x6, Pallas kernels: 7.46 us -> 5.26 us  [call(): pl.pallas_call(kernel, in_specs=[space for space, _ in operands], out_spe...]
    ppermute x1, waiting for transfers between devices: 0.01 us -> 0.52 us  [local(): got = lax.ppermute(send, 'row', SWAP)]
  transfers between devices with their start and end apart: 2 -> 2, of which waited for: 0 -> 1; matrix products, arithmetic and copies ran while one was open for 0% -> 0% of each run, Pallas kernels for 8% -> 6%
where the time goes in v5:
time: 47.6 us; the launch traced here: 47.4 us
  blocking collectives  36.2 us (76%)
  Pallas kernels  5.26 us (11%)
  starting transfers between devices  4.78 us (10%)
  between operations  0.69 us (1%)
  waiting for transfers between devices  0.52 us (1%)
    all_to_all x2, blocking collectives, exchange(): lax.all_to_all(message, 'col', 0, 0, tiled=True, axis_index_groups=[listed])  36.2 us
    pallas_call x6, Pallas kernels, call(): pl.pallas_call(kernel, in_specs=[space for space, _ in operands], out_spe...  5.26 us
    ppermute x1, starting transfers between devices, local(): got = lax.ppermute(send, 'row', SWAP)  3.32 us
    ppermute x1, starting transfers between devices, local(): other = lax.ppermute(features, 'row', SWAP)  1.46 us
  transfers between devices with their start and end apart: 2, of which 1 were waited for; matrix products, arithmetic and copies ran while one was open for 0% of the time, Pallas kernels for 6%

profile of v5, /device:TPU:1, one launch (start us, length us, event | category | flops | bytes accessed | tf_op | source)
XLA Modules:
  0.0 47.4 jit_solution(17830891716078721421)
XLA Ops:
  0.6 0.0 copy-start
  0.6 0.0 copy-start.1
  0.7 1.5 %collective-permute-start = (bf16[8,4096]{1,0:T(8,128)(2,1)}, bf16[8,4096]{1,0:T(8,128)(2,1)S(1)}, u32[]{:S(2)}, u32[]{:S(2)}) collective-permute-start(bf16[8,4096]{1,0:T(8,128)(2,1)} %own_hbm.1), channel_id=1, source_target_pairs={{0,64},{64,0},{1,65},{65,1},{2,66},{66,2},{3,67},{67,3},{4,68},{68... | collective-permute-start | bytes 196616 | tf_op jit(solution)/shard_map/ppermute | solution.py:236
  2.1 2.4 %first.1 = (s32[2,64,128]{2,1,0:T(8,128)S(1)}, bf16[32,2,2,128,128]{4,3,2,1,0:T(8,128)(2,1)S(1)}, f32[8,4096]{1,0:T(8,128)S(1)}) custom-call(s32[2,2,32]{2,1,0:T(2,128)} %bitcast.6, s32[2,32]{1,0:T(2,128)} %bitcast.7, bf16[8,4096]{1,0:T(8,128)(2,1)} %own_hbm.1, bf16[32,2,2,128,128]{4,3,2,1,0:T(8,128)(2,1)} %a_hbm.1), custom_call_target="tpu_custom_call" | custom-call | tf_op jit(solution)/shard_map/first/pallas_call | solution.py:216
  4.5 0.0 collective-permute-done.other
  4.5 0.0 copy-done
  4.5 0.0 copy-done.1
  4.5 0.7 %second.1 = bf16[64,8,512]{2,1,0:T(8,128)(2,1)S(1)} custom-call(s32[2,64,128]{2,1,0:T(8,128)S(1)} %get-tuple-element.11.table, bf16[8,4096]{1,0:T(8,128)(2,1)S(1)} %collective-permute-done.other, bf16[32,2,2,128,128]{4,3,2,1,0:T(8,128)(2,1)S(1)} %get-tuple-element.12.a_ref, f32[8,4096]{1,0:T(8,128)S(1)} %get-tuple-element.13.part, ...), custom_call_target="tpu_custom_call" | custom-call | tf_op jit(solution)/shard_map/second/pallas_call | solution.py:216
  5.2 20.5 %all_to_all.17 = bf16[64,8,512]{2,1,0:T(8,128)(2,1)S(1)} all-to-all(bf16[64,8,512]{2,1,0:T(8,128)(2,1)S(1)} %second.1), channel_id=1, replica_groups={{29,28,24,33,35,60,23,40,11,27,61,3,5,7,42,45,12,59,0,55,1,44,41,14,15,..., dimensions={0} | all-to-all | bytes 1048576 | tf_op jit(solution)/shard_map/all_to_all | solution.py:32
  25.7 0.5 %dense.1 = bf16[512,512]{1,0:T(8,128)(2,1)S(1)} custom-call(bf16[512,512]{1,0:T(8,128)(2,1)S(1)} %bitcast.4), custom_call_target="tpu_custom_call" | custom-call | tf_op jit(solution)/shard_map/dense/pallas_call | solution.py:216
  26.2 15.7 %all_to_all.18.back = bf16[64,8,512]{2,1,0:T(8,128)(2,1)S(1)} all-to-all(bf16[64,8,512]{2,1,0:T(8,128)(2,1)S(1)} %bitcast.5), channel_id=1, replica_groups={{29,28,24,33,35,60,23,40,11,27,61,3,5,7,42,45,12,59,0,55,1,44,41,14,15,..., dimensions={0} | all-to-all | bytes 1048576 | tf_op jit(solution)/shard_map/all_to_all | solution.py:32
  41.9 0.5 %send.1 = (f32[8,4608]{1,0:T(8,128)S(1)}, bf16[8,4096]{1,0:T(8,128)(2,1)S(1)}) custom-call(s32[2,64,128]{2,1,0:T(8,128)S(1)} %get-tuple-element.11.table, bf16[64,8,512]{2,1,0:T(8,128)(2,1)S(1)} %all_to_all.18.back, bf16[32,2,2,128,128]{4,3,2,1,0:T(8,128)(2,1)S(1)} %get-tuple-element.12.a_ref), custom_call_target="tpu_custom_call" | custom-call | tf_op jit(solution)/shard_map/send/pallas_call | solution.py:216
  42.4 3.3 %collective-permute-start.1 = (f32[8,4608]{1,0:T(8,128)S(1)}, f32[8,4608]{1,0:T(8,128)S(1)}, u32[]{:S(2)}, u32[]{:S(2)}) collective-permute-start(f32[8,4608]{1,0:T(8,128)S(1)} %get-tuple-element.15.sent), channel_id=1, source_target_pairs={{0,64},{64,0},{1,65},{65,1},{2,66},{66,2},{3,67},{67,3},{4,68},{68... | collective-permute-start | bytes 442376 | tf_op jit(solution)/shard_map/ppermute | solution.py:276
  45.7 0.5 %keep.1.own = f32[8,4224]{1,0:T(8,128)S(1)} custom-call(s32[2,64,128]{2,1,0:T(8,128)S(1)} %get-tuple-element.11.table, bf16[32,2,2,128,128]{4,3,2,1,0:T(8,128)(2,1)S(1)} %get-tuple-element.12.a_ref, bf16[8,4096]{1,0:T(8,128)(2,1)S(1)} %get-tuple-element.14.dagg_ref), custom_call_target="tpu_custom_call" | custom-call | tf_op jit(solution)/shard_map/keep/pallas_call | solution.py:216
  46.2 0.5 %collective-permute-done.1.got = f32[8,4608]{1,0:T(8,128)S(1)} collective-permute-done((f32[8,4608]{1,0:T(8,128)S(1)}, f32[8,4608]{1,0:T(8,128)S(1)}, u32[]{:S(2)}, u32[]{:S(2)}) %collective-permute-start.1) | collective-permute-done | bytes 147488 | tf_op jit(solution)/shard_map/ppermute | solution.py:276
  46.8 0.7 %merge.1 = (bf16[8,4096]{1,0:T(8,128)(2,1)}, bf16[8,4096]{1,0:T(8,128)(2,1)}, f32[8,512]{1,0:T(8,128)}) custom-call(bf16[64,8,512]{2,1,0:T(8,128)(2,1)S(1)} %all_to_all.18.back, f32[8,4224]{1,0:T(8,128)S(1)} %keep.1.own, f32[8,4608]{1,0:T(8,128)S(1)} %get-tuple-element.15.sent, f32[8,4608]{1,0:T(8,128)S(1)} %collective-permute-done.1.got), custom_call_target="tpu_custom_call" | custom-call | tf_op jit(solution)/shard_map/merge/pallas_call | solution.py:216
Async XLA Ops:
  0.6 3.9 %copy-start = (bf16[8,4096]{1,0:T(8,128)(2,1)S(1)}, bf16[8,4096]{1,0:T(8,128)(2,1)}, u32[]{:S(2)}) copy-start(bf16[8,4096]{1,0:T(8,128)(2,1)} %cot.1) | copy-start | bytes 196612
  0.6 3.9 %copy-start.1 = (bf16[8,512]{1,0:T(8,128)(2,1)S(1)}, bf16[8,512]{1,0:T(8,128)(2,1)}, u32[]{:S(2)}) copy-start(bf16[8,512]{1,0:T(8,128)(2,1)} %weight.1) | copy-start | bytes 24580
  0.7 3.9 %collective-permute-start = (bf16[8,4096]{1,0:T(8,128)(2,1)}, bf16[8,4096]{1,0:T(8,128)(2,1)S(1)}, u32[]{:S(2)}, u32[]{:S(2)}) collective-permute-start(bf16[8,4096]{1,0:T(8,128)(2,1)} %own_hbm.1), channel_id=1, source_target_pairs={{0,64},{64,0},{1,65},{65,1},{2,66},{66,2},{3,67},{67,3},{4,68},{68... | collective-permute-start | bytes 196616 | tf_op jit(solution)/shard_map/ppermute | solution.py:236
  42.4 4.3 %collective-permute-start.1 = (f32[8,4608]{1,0:T(8,128)S(1)}, f32[8,4608]{1,0:T(8,128)S(1)}, u32[]{:S(2)}, u32[]{:S(2)}) collective-permute-start(f32[8,4608]{1,0:T(8,128)S(1)} %get-tuple-element.15.sent), channel_id=1, source_target_pairs={{0,64},{64,0},{1,65},{65,1},{2,66},{66,2},{3,67},{67,3},{4,68},{68... | collective-permute-start | bytes 442376 | tf_op jit(solution)/shard_map/ppermute | solution.py:276

commit v6 on v5

--- a/solution.py
+++ b/solution.py
@@ -12,10 +12,10 @@
 CHUNKS = 4
 LANE = 128
 ORDER_SEED = (
-    29, 28, 24, 33, 35, 60, 23, 40, 11, 27, 61, 3, 5, 7, 42, 45,
-    12, 59, 0, 55, 1, 44, 41, 14, 15, 17, 47, 20, 63, 10, 62, 54,
-    36, 51, 21, 4, 43, 52, 9, 38, 34, 58, 39, 6, 46, 18, 8, 57,
-    13, 37, 22, 30, 19, 53, 50, 25, 31, 32, 16, 2, 26, 56, 48, 49,
+    58, 10, 56, 63, 55, 48, 4, 54, 34, 0, 3, 5, 27, 44, 50, 33,
+    14, 62, 30, 19, 42, 60, 12, 28, 24, 37, 61, 36, 47, 35, 45, 7,
+    8, 6, 41, 22, 51, 57, 46, 15, 39, 16, 52, 59, 49, 1, 13, 38,
+    31, 53, 2, 11, 20, 40, 29, 9, 17, 26, 21, 25, 23, 32, 18, 43,
 )
 
 

time: 47.6 us -> 45.4 us (0.954)
  starting transfers between devices: 4.78 us -> 3.32 us
  blocking collectives: 36.2 us -> 35.4 us
    ppermute x1, starting transfers between devices: 3.32 us -> 1.85 us  [local(): got = lax.ppermute(send, 'row', SWAP)]
    all_to_all x2, blocking collectives: 36.2 us -> 35.4 us  [exchange(): lax.all_to_all(message, 'col', 0, 0, tiled=True, axis_index_groups=[listed])]
where the time goes in v6:
time: 45.4 us; the launch traced here: 45.2 us
  blocking collectives  35.4 us (78%)
  Pallas kernels  5.33 us (12%)
  starting transfers between devices  3.32 us (7%)
  between operations  0.69 us (2%)
  waiting for transfers between devices  0.49 us (1%)
    all_to_all x2, blocking collectives, exchange(): lax.all_to_all(message, 'col', 0, 0, tiled=True, axis_index_groups=[listed])  35.4 us
    pallas_call x6, Pallas kernels, call(): pl.pallas_call(kernel, in_specs=[space for space, _ in operands], out_spe...  5.33 us
    ppermute x1, starting transfers between devices, local(): got = lax.ppermute(send, 'row', SWAP)  1.85 us
    ppermute x1, starting transfers between devices, local(): other = lax.ppermute(features, 'row', SWAP)  1.46 us
  transfers between devices with their start and end apart: 2, of which 1 were waited for; matrix products, arithmetic and copies ran while one was open for 0% of the time, Pallas kernels for 6%

profile of v6, /device:TPU:1, one launch (start us, length us, event | category | flops | bytes accessed | tf_op | source)
XLA Modules:
  0.0 45.2 jit_solution(11420259205433753596)
XLA Ops:
  0.6 0.0 copy-start
  0.6 0.0 copy-start.1
  0.7 1.5 %collective-permute-start = (bf16[8,4096]{1,0:T(8,128)(2,1)}, bf16[8,4096]{1,0:T(8,128)(2,1)S(1)}, u32[]{:S(2)}, u32[]{:S(2)}) collective-permute-start(bf16[8,4096]{1,0:T(8,128)(2,1)} %own_hbm.1), channel_id=1, source_target_pairs={{0,64},{64,0},{1,65},{65,1},{2,66},{66,2},{3,67},{67,3},{4,68},{68... | collective-permute-start | bytes 196616 | tf_op jit(solution)/shard_map/ppermute | solution.py:236
  2.1 2.4 %first.1 = (s32[2,64,128]{2,1,0:T(8,128)S(1)}, bf16[32,2,2,128,128]{4,3,2,1,0:T(8,128)(2,1)S(1)}, f32[8,4096]{1,0:T(8,128)S(1)}) custom-call(s32[2,2,32]{2,1,0:T(2,128)} %bitcast.6, s32[2,32]{1,0:T(2,128)} %bitcast.7, bf16[8,4096]{1,0:T(8,128)(2,1)} %own_hbm.1, bf16[32,2,2,128,128]{4,3,2,1,0:T(8,128)(2,1)} %a_hbm.1), custom_call_target="tpu_custom_call" | custom-call | tf_op jit(solution)/shard_map/first/pallas_call | solution.py:216
  4.5 0.0 collective-permute-done.other
  4.5 0.0 copy-done
  4.5 0.0 copy-done.1
  4.5 0.7 %second.1 = bf16[64,8,512]{2,1,0:T(8,128)(2,1)S(1)} custom-call(s32[2,64,128]{2,1,0:T(8,128)S(1)} %get-tuple-element.11.table, bf16[8,4096]{1,0:T(8,128)(2,1)S(1)} %collective-permute-done.other, bf16[32,2,2,128,128]{4,3,2,1,0:T(8,128)(2,1)S(1)} %get-tuple-element.12.a_ref, f32[8,4096]{1,0:T(8,128)S(1)} %get-tuple-element.13.part, ...), custom_call_target="tpu_custom_call" | custom-call | tf_op jit(solution)/shard_map/second/pallas_call | solution.py:216
  5.2 19.1 %all_to_all.17 = bf16[64,8,512]{2,1,0:T(8,128)(2,1)S(1)} all-to-all(bf16[64,8,512]{2,1,0:T(8,128)(2,1)S(1)} %second.1), channel_id=1, replica_groups={{58,10,56,63,55,48,4,54,34,0,3,5,27,44,50,33,14,62,30,19,42,60,12,28,24..., dimensions={0} | all-to-all | bytes 1048576 | tf_op jit(solution)/shard_map/all_to_all | solution.py:32
  24.4 0.5 %dense.1 = bf16[512,512]{1,0:T(8,128)(2,1)S(1)} custom-call(bf16[512,512]{1,0:T(8,128)(2,1)S(1)} %bitcast.4), custom_call_target="tpu_custom_call" | custom-call | tf_op jit(solution)/shard_map/dense/pallas_call | solution.py:216
  24.9 16.2 %all_to_all.18.back = bf16[64,8,512]{2,1,0:T(8,128)(2,1)S(1)} all-to-all(bf16[64,8,512]{2,1,0:T(8,128)(2,1)S(1)} %bitcast.5), channel_id=1, replica_groups={{58,10,56,63,55,48,4,54,34,0,3,5,27,44,50,33,14,62,30,19,42,60,12,28,24..., dimensions={0} | all-to-all | bytes 1048576 | tf_op jit(solution)/shard_map/all_to_all | solution.py:32
  41.1 0.5 %send.1 = (f32[8,4608]{1,0:T(8,128)S(1)}, bf16[8,4096]{1,0:T(8,128)(2,1)S(1)}) custom-call(s32[2,64,128]{2,1,0:T(8,128)S(1)} %get-tuple-element.11.table, bf16[64,8,512]{2,1,0:T(8,128)(2,1)S(1)} %all_to_all.18.back, bf16[32,2,2,128,128]{4,3,2,1,0:T(8,128)(2,1)S(1)} %get-tuple-element.12.a_ref), custom_call_target="tpu_custom_call" | custom-call | tf_op jit(solution)/shard_map/send/pallas_call | solution.py:216
  41.7 1.9 %collective-permute-start.1 = (f32[8,4608]{1,0:T(8,128)S(1)}, f32[8,4608]{1,0:T(8,128)S(1)}, u32[]{:S(2)}, u32[]{:S(2)}) collective-permute-start(f32[8,4608]{1,0:T(8,128)S(1)} %get-tuple-element.15.sent), channel_id=1, source_target_pairs={{0,64},{64,0},{1,65},{65,1},{2,66},{66,2},{3,67},{67,3},{4,68},{68... | collective-permute-start | bytes 442376 | tf_op jit(solution)/shard_map/ppermute | solution.py:276
  43.5 0.5 %keep.1.own = f32[8,4224]{1,0:T(8,128)S(1)} custom-call(s32[2,64,128]{2,1,0:T(8,128)S(1)} %get-tuple-element.11.table, bf16[32,2,2,128,128]{4,3,2,1,0:T(8,128)(2,1)S(1)} %get-tuple-element.12.a_ref, bf16[8,4096]{1,0:T(8,128)(2,1)S(1)} %get-tuple-element.14.dagg_ref), custom_call_target="tpu_custom_call" | custom-call | tf_op jit(solution)/shard_map/keep/pallas_call | solution.py:216
  44.0 0.5 %collective-permute-done.1.got = f32[8,4608]{1,0:T(8,128)S(1)} collective-permute-done((f32[8,4608]{1,0:T(8,128)S(1)}, f32[8,4608]{1,0:T(8,128)S(1)}, u32[]{:S(2)}, u32[]{:S(2)}) %collective-permute-start.1) | collective-permute-done | bytes 147488 | tf_op jit(solution)/shard_map/ppermute | solution.py:276
  44.5 0.7 %merge.1 = (bf16[8,4096]{1,0:T(8,128)(2,1)}, bf16[8,4096]{1,0:T(8,128)(2,1)}, f32[8,512]{1,0:T(8,128)}) custom-call(bf16[64,8,512]{2,1,0:T(8,128)(2,1)S(1)} %all_to_all.18.back, f32[8,4224]{1,0:T(8,128)S(1)} %keep.1.own, f32[8,4608]{1,0:T(8,128)S(1)} %get-tuple-element.15.sent, f32[8,4608]{1,0:T(8,128)S(1)} %collective-permute-done.1.got), custom_call_target="tpu_custom_call" | custom-call | tf_op jit(solution)/shard_map/merge/pallas_call | solution.py:216
Async XLA Ops:
  0.6 3.9 %copy-start = (bf16[8,4096]{1,0:T(8,128)(2,1)S(1)}, bf16[8,4096]{1,0:T(8,128)(2,1)}, u32[]{:S(2)}) copy-start(bf16[8,4096]{1,0:T(8,128)(2,1)} %cot.1) | copy-start | bytes 196612
  0.6 3.9 %copy-start.1 = (bf16[8,512]{1,0:T(8,128)(2,1)S(1)}, bf16[8,512]{1,0:T(8,128)(2,1)}, u32[]{:S(2)}) copy-start(bf16[8,512]{1,0:T(8,128)(2,1)} %weight.1) | copy-start | bytes 24580
  0.7 3.9 %collective-permute-start = (bf16[8,4096]{1,0:T(8,128)(2,1)}, bf16[8,4096]{1,0:T(8,128)(2,1)S(1)}, u32[]{:S(2)}, u32[]{:S(2)}) collective-permute-start(bf16[8,4096]{1,0:T(8,128)(2,1)} %own_hbm.1), channel_id=1, source_target_pairs={{0,64},{64,0},{1,65},{65,1},{2,66},{66,2},{3,67},{67,3},{4,68},{68... | collective-permute-start | bytes 196616 | tf_op jit(solution)/shard_map/ppermute | solution.py:236
  41.7 2.9 %collective-permute-start.1 = (f32[8,4608]{1,0:T(8,128)S(1)}, f32[8,4608]{1,0:T(8,128)S(1)}, u32[]{:S(2)}, u32[]{:S(2)}) collective-permute-start(f32[8,4608]{1,0:T(8,128)S(1)} %get-tuple-element.15.sent), channel_id=1, source_target_pairs={{0,64},{64,0},{1,65},{65,1},{2,66},{66,2},{3,67},{67,3},{4,68},{68... | collective-permute-start | bytes 442376 | tf_op jit(solution)/shard_map/ppermute | solution.py:276

commit v7 on v6

--- a/solution.py
+++ b/solution.py
@@ -30,15 +30,6 @@
 def exchange(message):
     listed, _ = order(lax.axis_size("col"))
     return lax.all_to_all(message, "col", 0, 0, tiled=True, axis_index_groups=[listed])
-
-
-def upper(shape):
-    return lax.broadcasted_iota(jnp.int32, shape, len(shape) - 2) % 8 < 4
-
-
-def swap_rows(x):
-    tiles = x.reshape(x.shape[0] // 8, 8, x.shape[1])
-    return pltpu.roll(tiles, 4, 1).reshape(x.shape)
 
 
 def aggregate(picked, a_ref, s, b):
@@ -118,73 +109,70 @@
     slab = other.shape[1]
     feats[:, :slab] = other[...]
     feats[:, slab:] = jnp.zeros((8, LANE), feats.dtype)
-    half = weight.shape[1] // 2
-    low = weight[:, :half].astype(jnp.float32)
-    high = weight[:, half:].astype(jnp.float32)
-    mask = upper(low.shape)
-    w = (
-        jnp.where(mask, low, swap_rows(high)).astype(jnp.bfloat16),
-        jnp.where(mask, swap_rows(low), high).astype(jnp.bfloat16),
-    )
+    w = two(weight[...])
     for b in range(a_ref.shape[0]):
         here = slice(b * LANE, (b + 1) * LANE)
         picked = [feats[:, column(table, 1 - row, k, b)] for k in range(2)]
-        total = part[:, here] + aggregate(picked, a_ref, 1 - row, b)
-        total = total.astype(jnp.bfloat16)
-        c = cot[:, here]
-        c = (c, swap_rows(c.astype(jnp.float32)).astype(jnp.bfloat16))
+        low, high = two(part[:, here] + aggregate(picked, a_ref, 1 - row, b))
+        c = two(cot[:, here])
         for q in range(2):
             slot = slots[2 * b + q]
-            msg[slot, :, :LANE] = total
-            msg[slot, :, LANE : 2 * LANE] = c[q]
-            msg[slot, :, 2 * LANE :] = w[q]
+            msg[slot, :, :LANE] = low
+            msg[slot, :, LANE : 2 * LANE] = high
+            msg[slot, :, 2 * LANE : 3 * LANE] = c[q]
+            msg[slot, :, 3 * LANE :] = w[q]
+
+
+def two(x):
+    x = x.astype(jnp.float32)
+    return x[:4].astype(jnp.bfloat16), x[4:].astype(jnp.bfloat16)
+
+
+def rows(x):
+    return x.astype(jnp.float32).reshape(-1, x.shape[-1])
 
 
 def dense_kernel(slots, msg, back):
-    half = len(slots) // 2
-    tiles = [msg[8 * slot : 8 * slot + 8, :LANE].astype(jnp.float32) for slot in slots]
     agg = jnp.concatenate(
-        [jnp.concatenate(tiles[:half], 0), jnp.concatenate(tiles[half:], 0)], 1
+        [
+            msg[slot, :, half * LANE : (half + 1) * LANE].astype(jnp.float32)
+            for slot in slots
+            for half in range(2)
+        ],
+        0,
     ).astype(jnp.bfloat16)
-    w = msg[:, 2 * LANE :]
+    w = rows(msg[:, :, 3 * LANE :]).astype(jnp.bfloat16)
     pre = jnp.dot(w, agg, preferred_element_type=jnp.float32)
-    pre = pre[:, :LANE] + swap_rows(pre[:, LANE:])
-    cot = msg[:, LANE : 2 * LANE].astype(jnp.float32)
+    cot = rows(msg[:, :, 2 * LANE : 3 * LANE])
     sig = jax.nn.sigmoid(pre)
-    back[:, LANE : 2 * LANE] = (pre * sig).astype(jnp.bfloat16)
-    dpre = cot * sig * (1.0 + pre * (1.0 - sig))
-    dpre = jnp.where(upper(dpre.shape), dpre, 0.0)
-    dpre = jnp.concatenate([dpre, swap_rows(dpre)], 1).astype(jnp.bfloat16)
+    tiles = (len(slots), 4, -1)
+    back[:, :, 2 * LANE : 3 * LANE] = (pre * sig).reshape(tiles).astype(jnp.bfloat16)
+    dpre = (cot * sig * (1.0 + pre * (1.0 - sig))).astype(jnp.bfloat16)
     dagg = lax.dot_general(w, dpre, (((0,), (0,)), ((), ())), preferred_element_type=jnp.float32)
     for device, slot in enumerate(slots):
-        rows = (device % half) * 8
-        lanes = (device // half) * LANE
-        back[8 * slot : 8 * slot + 8, :LANE] = dagg[rows : rows + 8, lanes : lanes + LANE].astype(
-            jnp.bfloat16
-        )
+        low, high = two(dagg[8 * device : 8 * device + 8])
+        back[slot, :, :LANE] = low
+        back[slot, :, LANE : 2 * LANE] = high
     grad = lax.dot_general(dpre, agg, (((1,), (1,)), ((), ())), preferred_element_type=jnp.float32)
-    back[:, 2 * LANE :] = grad.astype(jnp.bfloat16)
+    back[:, :, 3 * LANE :] = grad.reshape(tiles).astype(jnp.bfloat16)
 
 
 def send_kernel(slots, table, back, a_ref, send, dagg_ref):
     row = lax.axis_index("row")
     blocks = a_ref.shape[0]
     slab = blocks * LANE
-    half = (send.shape[1] - slab) // 2
     send[...] = jnp.zeros_like(send)
-    grads = [jnp.zeros((8, half), jnp.float32) for _ in range(2)]
+    grads = [jnp.zeros((4, send.shape[1] - slab), jnp.float32) for _ in range(2)]
     for b in range(blocks):
-        dagg = jnp.zeros((8, LANE), jnp.float32)
+        dagg = jnp.zeros((4, 2 * LANE), jnp.float32)
         for q in range(2):
             tile = back.at[slots[2 * b + q]]
-            dagg += tile[:, :LANE].astype(jnp.float32)
-            grads[q] += tile[:, 2 * LANE :].astype(jnp.float32)
-        dagg = dagg.astype(jnp.bfloat16)
+            dagg += tile[:, : 2 * LANE].astype(jnp.float32)
+            grads[q] += tile[:, 3 * LANE :].astype(jnp.float32)
+        dagg = jnp.concatenate([dagg[:, :LANE], dagg[:, LANE:]], 0).astype(jnp.bfloat16)
         dagg_ref[:, b * LANE : (b + 1) * LANE] = dagg
         spread(table, dagg, a_ref, 1 - row, b, send)
-    mask = upper((8, half))
-    send[:, slab : slab + half] = jnp.where(mask, grads[0], swap_rows(grads[1]))
-    send[:, slab + half :] = jnp.where(mask, swap_rows(grads[0]), grads[1])
+    send[:, slab:] = jnp.concatenate(grads, 0)
 
 
 def keep_kernel(table, a_ref, dagg_ref, own):
@@ -196,14 +184,11 @@
 
 
 def merge_kernel(slots, scale, back, own, sent, got, out, grad_features, grad_weight):
-    mask = upper((8, LANE))
     for b in range(len(slots) // 2):
-        first, second = (
-            back[slots[2 * b + q], :, LANE : 2 * LANE].astype(jnp.float32) for q in range(2)
-        )
-        out[:, b * LANE : (b + 1) * LANE] = jnp.where(mask, first, swap_rows(second)).astype(
-            jnp.bfloat16
-        )
+        tiles = [
+            back[slots[2 * b + q], :, 2 * LANE : 3 * LANE].astype(jnp.float32) for q in range(2)
+        ]
+        out[:, b * LANE : (b + 1) * LANE] = jnp.concatenate(tiles, 0).astype(jnp.bfloat16)
     slab = grad_features.shape[1]
     grad_features[...] = (own[:, :slab] + got[:, :slab]).astype(jnp.bfloat16)
     grad_weight[...] = (sent[:, slab:] + got[:, slab:]) * scale
@@ -227,7 +212,7 @@
 def local(features, a_blocks, block_cols, block_counts, weight, cotangent):
     fd, slab = features.shape
     width = weight.shape[1]
-    lanes = 2 * LANE + width // 2
+    lanes = 3 * LANE + width
     ranks = lax.axis_size("col")
     slots = order(ranks)[1]
     cols, counts = block_cols.transpose(1, 2, 0), block_counts.transpose(1, 0)
@@ -259,14 +244,14 @@
         functools.partial(second_kernel, slots),
         "second",
         [(VMEM, table)] + [(VMEM, x) for x in (other, blocks, part, weight, cotangent)],
-        [(VMEM, (ranks, fd, lanes), bf16)],
+        [(VMEM, (ranks, fd // 2, lanes), bf16)],
         [pltpu.VMEM((fd, slab + LANE), bf16)],
     )
-    msg = exchange(msg.reshape(ranks * fd, lanes))
+    msg = exchange(msg)
     (back,) = call(
         functools.partial(dense_kernel, slots), "dense", [(VMEM, msg)], [(VMEM, msg.shape, bf16)]
     )
-    back = exchange(back).reshape(ranks, fd, lanes)
+    back = exchange(back)
     send, dagg = call(
         functools.partial(send_kernel, slots),
         "send",

time: 45.4 us -> 44.1 us (0.971)
  blocking collectives: 35.4 us -> 33.1 us
  starting transfers between devices: 3.32 us -> 4.26 us
    all_to_all x2, blocking collectives: 35.4 us -> 33.1 us  [exchange(): lax.all_to_all(message, 'col', 0, 0, tiled=True, axis_index_groups=[listed])]
    ppermute x1, starting transfers between devices: 1.85 us -> 2.8 us  [local(): got = lax.ppermute(send, 'row', SWAP)]
  transfers between devices with their start and end apart: 2 -> 2, of which waited for: 1 -> 1; matrix products, arithmetic and copies ran while one was open for 0% -> 0% of each run, Pallas kernels for 6% -> 7%
where the time goes in v7:
time: 44.1 us; the launch traced here: 43.9 us
  blocking collectives  33.1 us (75%)
  Pallas kernels  5.36 us (12%)
  starting transfers between devices  4.26 us (10%)
  between operations  0.69 us (2%)
  waiting for transfers between devices  0.5 us (1%)
    all_to_all x2, blocking collectives, exchange(): lax.all_to_all(message, 'col', 0, 0, tiled=True, axis_index_groups=[listed])  33.1 us
    pallas_call x6, Pallas kernels, call(): pl.pallas_call(kernel, in_specs=[space for space, _ in operands], out_spe...  5.36 us
    ppermute x1, starting transfers between devices, local(): got = lax.ppermute(send, 'row', SWAP)  2.8 us
    ppermute x1, starting transfers between devices, local(): other = lax.ppermute(features, 'row', SWAP)  1.46 us
  transfers between devices with their start and end apart: 2, of which 1 were waited for; matrix products, arithmetic and copies ran while one was open for 0% of the time, Pallas kernels for 7%

profile of v7, /device:TPU:1, one launch (start us, length us, event | category | flops | bytes accessed | tf_op | source)
XLA Modules:
  0.0 43.9 jit_solution(13969375667536457564)
XLA Ops:
  0.6 0.0 copy-start
  0.6 0.0 copy-start.1
  0.7 1.5 %collective-permute-start = (bf16[8,4096]{1,0:T(8,128)(2,1)}, bf16[8,4096]{1,0:T(8,128)(2,1)S(1)}, u32[]{:S(2)}, u32[]{:S(2)}) collective-permute-start(bf16[8,4096]{1,0:T(8,128)(2,1)} %own_hbm.1), channel_id=1, source_target_pairs={{0,64},{64,0},{1,65},{65,1},{2,66},{66,2},{3,67},{67,3},{4,68},{68... | collective-permute-start | bytes 196616 | tf_op jit(solution)/shard_map/ppermute | solution.py:221
  2.1 2.4 %first.1 = (s32[2,64,128]{2,1,0:T(8,128)S(1)}, bf16[32,2,2,128,128]{4,3,2,1,0:T(8,128)(2,1)S(1)}, f32[8,4096]{1,0:T(8,128)S(1)}) custom-call(s32[2,2,32]{2,1,0:T(2,128)} %bitcast.2, s32[2,32]{1,0:T(2,128)} %bitcast.3, bf16[8,4096]{1,0:T(8,128)(2,1)} %own_hbm.1, bf16[32,2,2,128,128]{4,3,2,1,0:T(8,128)(2,1)} %a_hbm.1), custom_call_target="tpu_custom_call" | custom-call | tf_op jit(solution)/shard_map/first/pallas_call | solution.py:201
  4.5 0.0 collective-permute-done.other
  4.5 0.0 copy-done
  4.5 0.0 copy-done.1
  4.5 0.7 %second.1 = bf16[64,4,896]{2,1,0:T(4,128)(2,1)S(1)} custom-call(s32[2,64,128]{2,1,0:T(8,128)S(1)} %get-tuple-element.11.table, bf16[8,4096]{1,0:T(8,128)(2,1)S(1)} %collective-permute-done.other, bf16[32,2,2,128,128]{4,3,2,1,0:T(8,128)(2,1)S(1)} %get-tuple-element.12.a_ref, f32[8,4096]{1,0:T(8,128)S(1)} %get-tuple-element.13.part, ...), custom_call_target="tpu_custom_call" | custom-call | tf_op jit(solution)/shard_map/second/pallas_call | solution.py:201
  5.3 18.3 %all_to_all.10.msg = bf16[64,4,896]{2,1,0:T(4,128)(2,1)S(1)} all-to-all(bf16[64,4,896]{2,1,0:T(4,128)(2,1)S(1)} %second.1), channel_id=1, replica_groups={{58,10,56,63,55,48,4,54,34,0,3,5,27,44,50,33,14,62,30,19,42,60,12,28,24..., dimensions={0} | all-to-all | bytes 917504 | tf_op jit(solution)/shard_map/all_to_all | solution.py:32
  23.6 0.5 %dense.1 = bf16[64,4,896]{2,1,0:T(4,128)(2,1)S(1)} custom-call(bf16[64,4,896]{2,1,0:T(4,128)(2,1)S(1)} %all_to_all.10.msg), custom_call_target="tpu_custom_call" | custom-call | tf_op jit(solution)/shard_map/dense/pallas_call | solution.py:201
  24.2 14.8 %all_to_all.11.back = bf16[64,4,896]{2,1,0:T(4,128)(2,1)S(1)} all-to-all(bf16[64,4,896]{2,1,0:T(4,128)(2,1)S(1)} %dense.1), channel_id=1, replica_groups={{58,10,56,63,55,48,4,54,34,0,3,5,27,44,50,33,14,62,30,19,42,60,12,28,24..., dimensions={0} | all-to-all | bytes 917504 | tf_op jit(solution)/shard_map/all_to_all | solution.py:32
  38.9 0.5 %send.1 = (f32[8,4608]{1,0:T(8,128)S(1)}, bf16[8,4096]{1,0:T(8,128)(2,1)S(1)}) custom-call(s32[2,64,128]{2,1,0:T(8,128)S(1)} %get-tuple-element.11.table, bf16[64,4,896]{2,1,0:T(4,128)(2,1)S(1)} %all_to_all.11.back, bf16[32,2,2,128,128]{4,3,2,1,0:T(8,128)(2,1)S(1)} %get-tuple-element.12.a_ref), custom_call_target="tpu_custom_call" | custom-call | tf_op jit(solution)/shard_map/send/pallas_call | solution.py:201
  39.4 2.8 %collective-permute-start.1 = (f32[8,4608]{1,0:T(8,128)S(1)}, f32[8,4608]{1,0:T(8,128)S(1)}, u32[]{:S(2)}, u32[]{:S(2)}) collective-permute-start(f32[8,4608]{1,0:T(8,128)S(1)} %get-tuple-element.15.sent), channel_id=1, source_target_pairs={{0,64},{64,0},{1,65},{65,1},{2,66},{66,2},{3,67},{67,3},{4,68},{68... | collective-permute-start | bytes 442376 | tf_op jit(solution)/shard_map/ppermute | solution.py:261
  42.2 0.5 %keep.1.own = f32[8,4224]{1,0:T(8,128)S(1)} custom-call(s32[2,64,128]{2,1,0:T(8,128)S(1)} %get-tuple-element.11.table, bf16[32,2,2,128,128]{4,3,2,1,0:T(8,128)(2,1)S(1)} %get-tuple-element.12.a_ref, bf16[8,4096]{1,0:T(8,128)(2,1)S(1)} %get-tuple-element.14.dagg_ref), custom_call_target="tpu_custom_call" | custom-call | tf_op jit(solution)/shard_map/keep/pallas_call | solution.py:201
  42.7 0.5 %collective-permute-done.1.got = f32[8,4608]{1,0:T(8,128)S(1)} collective-permute-done((f32[8,4608]{1,0:T(8,128)S(1)}, f32[8,4608]{1,0:T(8,128)S(1)}, u32[]{:S(2)}, u32[]{:S(2)}) %collective-permute-start.1) | collective-permute-done | bytes 147488 | tf_op jit(solution)/shard_map/ppermute | solution.py:261
  43.2 0.7 %merge.1 = (bf16[8,4096]{1,0:T(8,128)(2,1)}, bf16[8,4096]{1,0:T(8,128)(2,1)}, f32[8,512]{1,0:T(8,128)}) custom-call(bf16[64,4,896]{2,1,0:T(4,128)(2,1)S(1)} %all_to_all.11.back, f32[8,4224]{1,0:T(8,128)S(1)} %keep.1.own, f32[8,4608]{1,0:T(8,128)S(1)} %get-tuple-element.15.sent, f32[8,4608]{1,0:T(8,128)S(1)} %collective-permute-done.1.got), custom_call_target="tpu_custom_call" | custom-call | tf_op jit(solution)/shard_map/merge/pallas_call | solution.py:201
Async XLA Ops:
  0.6 3.9 %copy-start = (bf16[8,4096]{1,0:T(8,128)(2,1)S(1)}, bf16[8,4096]{1,0:T(8,128)(2,1)}, u32[]{:S(2)}) copy-start(bf16[8,4096]{1,0:T(8,128)(2,1)} %cot.1) | copy-start | bytes 196612
  0.6 3.9 %copy-start.1 = (bf16[8,512]{1,0:T(8,128)(2,1)S(1)}, bf16[8,512]{1,0:T(8,128)(2,1)}, u32[]{:S(2)}) copy-start(bf16[8,512]{1,0:T(8,128)(2,1)} %weight.1) | copy-start | bytes 24580
  0.7 3.9 %collective-permute-start = (bf16[8,4096]{1,0:T(8,128)(2,1)}, bf16[8,4096]{1,0:T(8,128)(2,1)S(1)}, u32[]{:S(2)}, u32[]{:S(2)}) collective-permute-start(bf16[8,4096]{1,0:T(8,128)(2,1)} %own_hbm.1), channel_id=1, source_target_pairs={{0,64},{64,0},{1,65},{65,1},{2,66},{66,2},{3,67},{67,3},{4,68},{68... | collective-permute-start | bytes 196616 | tf_op jit(solution)/shard_map/ppermute | solution.py:221
  39.4 3.8 %collective-permute-start.1 = (f32[8,4608]{1,0:T(8,128)S(1)}, f32[8,4608]{1,0:T(8,128)S(1)}, u32[]{:S(2)}, u32[]{:S(2)}) collective-permute-start(f32[8,4608]{1,0:T(8,128)S(1)} %get-tuple-element.15.sent), channel_id=1, source_target_pairs={{0,64},{64,0},{1,65},{65,1},{2,66},{66,2},{3,67},{67,3},{4,68},{68... | collective-permute-start | bytes 442376 | tf_op jit(solution)/shard_map/ppermute | solution.py:261

commit v8 on v7

--- a/solution.py
+++ b/solution.py
@@ -11,6 +11,7 @@
 VMEM_LIMIT = 4 << 20
 CHUNKS = 4
 LANE = 128
+BUFFERS = 2
 ORDER_SEED = (
     58, 10, 56, 63, 55, 48, 4, 54, 34, 0, 3, 5, 27, 44, 50, 33,
     14, 62, 30, 19, 42, 60, 12, 28, 24, 37, 61, 36, 47, 35, 45, 7,
@@ -48,7 +49,8 @@
         preferred_element_type=jnp.float32,
     )
     for k in range(2):
-        terms[:, column(table, s, k, b)] += both[:, k * LANE : (k + 1) * LANE]
+        buffer = terms[(2 * b + k) % len(terms)]
+        buffer[:, column(table, s, k, b)] += both[:, k * LANE : (k + 1) * LANE]
 
 
 def column(table, s, k, b):
@@ -56,7 +58,25 @@
 
 
 def first_kernel(
-    cols_hbm, counts_hbm, own_hbm, a_hbm, columns, a_ref, total, own, cols, counts, table, scalars, sems
+    slots,
+    cols_hbm,
+    counts_hbm,
+    own_hbm,
+    weight_hbm,
+    cot_hbm,
+    a_hbm,
+    columns,
+    a_ref,
+    total,
+    msg,
+    own,
+    weight,
+    cot,
+    cols,
+    counts,
+    table,
+    scalars,
+    sems,
 ):
     row = lax.axis_index("row")
     blocks = a_ref.shape[0]
@@ -65,7 +85,13 @@
     small = [
         pltpu.make_async_copy(src, dst, sems.at[i])
         for i, (src, dst) in enumerate(
-            ((cols_hbm, cols), (counts_hbm, counts), (own_hbm, own.at[:, pl.ds(0, slab)]))
+            (
+                (cols_hbm, cols),
+                (counts_hbm, counts),
+                (own_hbm, own.at[:, pl.ds(0, slab)]),
+                (weight_hbm, weight),
+                (cot_hbm, cot),
+            )
         )
     ]
     large = []
@@ -100,27 +126,33 @@
         for k in range(2):
             for b in range(blocks):
                 columns[s, k * blocks + b, :] = jnp.full((LANE,), scalars[s, k, b], jnp.int32)
+    small[3].wait()
+    small[4].wait()
+    w = two(weight[...])
+    for b in range(blocks):
+        c = two(cot[:, b * LANE : (b + 1) * LANE])
+        for q in range(2):
+            slot = slots[2 * b + q]
+            msg[slot, :, 2 * LANE : 3 * LANE] = c[q]
+            msg[slot, :, 3 * LANE :] = w[q]
     for copy in large[CHUNKS:]:
         copy.wait()
 
 
-def second_kernel(slots, table, other, a_ref, part, weight, cot, msg, feats):
+def second_kernel(slots, table, other, a_ref, part, begun, msg, feats):
+    del begun
     row = lax.axis_index("row")
     slab = other.shape[1]
     feats[:, :slab] = other[...]
     feats[:, slab:] = jnp.zeros((8, LANE), feats.dtype)
-    w = two(weight[...])
     for b in range(a_ref.shape[0]):
         here = slice(b * LANE, (b + 1) * LANE)
         picked = [feats[:, column(table, 1 - row, k, b)] for k in range(2)]
         low, high = two(part[:, here] + aggregate(picked, a_ref, 1 - row, b))
-        c = two(cot[:, here])
         for q in range(2):
             slot = slots[2 * b + q]
             msg[slot, :, :LANE] = low
             msg[slot, :, LANE : 2 * LANE] = high
-            msg[slot, :, 2 * LANE : 3 * LANE] = c[q]
-            msg[slot, :, 3 * LANE :] = w[q]
 
 
 def two(x):
@@ -141,7 +173,7 @@
         ],
         0,
     ).astype(jnp.bfloat16)
-    w = rows(msg[:, :, 3 * LANE :]).astype(jnp.bfloat16)
+    w = msg[:, :, 3 * LANE :].reshape(4 * len(slots), -1)
     pre = jnp.dot(w, agg, preferred_element_type=jnp.float32)
     cot = rows(msg[:, :, 2 * LANE : 3 * LANE])
     sig = jax.nn.sigmoid(pre)
@@ -154,14 +186,15 @@
         back[slot, :, :LANE] = low
         back[slot, :, LANE : 2 * LANE] = high
     grad = lax.dot_general(dpre, agg, (((1,), (1,)), ((), ())), preferred_element_type=jnp.float32)
-    back[:, :, 3 * LANE :] = grad.reshape(tiles).astype(jnp.bfloat16)
-
-
-def send_kernel(slots, table, back, a_ref, send, dagg_ref):
+    back[:, :, 3 * LANE :] = grad.astype(jnp.bfloat16).reshape(tiles)
+
+
+def send_kernel(slots, table, back, a_ref, send, dagg_ref, *more):
     row = lax.axis_index("row")
     blocks = a_ref.shape[0]
     slab = blocks * LANE
-    send[...] = jnp.zeros_like(send)
+    for buffer in (send, *more):
+        buffer[...] = jnp.zeros_like(buffer)
     grads = [jnp.zeros((4, send.shape[1] - slab), jnp.float32) for _ in range(2)]
     for b in range(blocks):
         dagg = jnp.zeros((4, 2 * LANE), jnp.float32)
@@ -171,39 +204,49 @@
             grads[q] += tile[:, 3 * LANE :].astype(jnp.float32)
         dagg = jnp.concatenate([dagg[:, :LANE], dagg[:, LANE:]], 0).astype(jnp.bfloat16)
         dagg_ref[:, b * LANE : (b + 1) * LANE] = dagg
-        spread(table, dagg, a_ref, 1 - row, b, send)
+        spread(table, dagg, a_ref, 1 - row, b, (send, *more))
+    total = send[:, :slab]
+    for buffer in more:
+        total += buffer[:, :slab]
+    send[:, :slab] = total
     send[:, slab:] = jnp.concatenate(grads, 0)
 
 
-def keep_kernel(table, a_ref, dagg_ref, own):
+def keep_kernel(table, a_ref, dagg_ref, *own):
     row = lax.axis_index("row")
     blocks = a_ref.shape[0]
-    own[...] = jnp.zeros_like(own)
+    for buffer in own:
+        buffer[...] = jnp.zeros_like(buffer)
     for b in range(blocks):
         spread(table, dagg_ref[:, b * LANE : (b + 1) * LANE], a_ref, row, b, own)
 
 
-def merge_kernel(slots, scale, back, own, sent, got, out, grad_features, grad_weight):
+def merge_kernel(slots, scale, back, sent, got, *refs):
+    own, (out, grad_features, grad_weight) = refs[:-3], refs[-3:]
     for b in range(len(slots) // 2):
         tiles = [
             back[slots[2 * b + q], :, 2 * LANE : 3 * LANE].astype(jnp.float32) for q in range(2)
         ]
         out[:, b * LANE : (b + 1) * LANE] = jnp.concatenate(tiles, 0).astype(jnp.bfloat16)
     slab = grad_features.shape[1]
-    grad_features[...] = (own[:, :slab] + got[:, :slab]).astype(jnp.bfloat16)
+    total = got[:, :slab]
+    for buffer in own:
+        total += buffer[:, :slab]
+    grad_features[...] = total.astype(jnp.bfloat16)
     grad_weight[...] = (sent[:, slab:] + got[:, slab:]) * scale
 
 
 HBM, VMEM = (pl.BlockSpec(memory_space=m) for m in (pltpu.HBM, pltpu.VMEM))
 
 
-def call(kernel, name, operands, outs, scratch=()):
+def call(kernel, name, operands, outs, scratch=(), aliases=None):
     return pl.pallas_call(
         kernel,
         in_specs=[space for space, _ in operands],
         out_specs=[space for space, _, _ in outs],
         out_shape=[jax.ShapeDtypeStruct(shape, dtype) for _, shape, dtype in outs],
         scratch_shapes=list(scratch),
+        input_output_aliases=aliases or {},
         compiler_params=pltpu.CompilerParams(vmem_limit_bytes=VMEM_LIMIT),
         name=name,
     )(*(array for _, array in operands))
@@ -219,33 +262,37 @@
     bf16, f32, i32 = jnp.bfloat16, jnp.float32, jnp.int32
 
     other = lax.ppermute(features, "row", SWAP)
-    table, blocks, part = call(
-        first_kernel,
+    table, blocks, part, msg = call(
+        functools.partial(first_kernel, slots),
         "first",
         [
             (HBM, pltpu.with_memory_space_constraint(x, pltpu.HBM))
-            for x in (cols, counts, features, a_blocks)
+            for x in (cols, counts, features, weight, cotangent, a_blocks)
         ],
         [
             (VMEM, (2, 2 * cols.shape[2], LANE), i32),
             (VMEM, a_blocks.shape, bf16),
             (VMEM, (fd, slab), f32),
+            (VMEM, (ranks, fd // 2, lanes), bf16),
         ],
         [
             pltpu.VMEM((fd, slab + LANE), bf16),
+            pltpu.VMEM(weight.shape, bf16),
+            pltpu.VMEM(cotangent.shape, bf16),
             pltpu.VMEM(cols.shape, i32),
             pltpu.VMEM(counts.shape, i32),
             pltpu.VMEM(cols.shape, i32),
             pltpu.SMEM(cols.shape, i32),
-            pltpu.SemaphoreType.DMA((3 + 2 * CHUNKS,)),
+            pltpu.SemaphoreType.DMA((5 + 2 * CHUNKS,)),
         ],
     )
     (msg,) = call(
         functools.partial(second_kernel, slots),
         "second",
-        [(VMEM, table)] + [(VMEM, x) for x in (other, blocks, part, weight, cotangent)],
+        [(VMEM, x) for x in (table, other, blocks, part, msg)],
         [(VMEM, (ranks, fd // 2, lanes), bf16)],
         [pltpu.VMEM((fd, slab + LANE), bf16)],
+        {4: 0},
     )
     msg = exchange(msg)
     (back,) = call(
@@ -257,19 +304,20 @@
         "send",
         [(VMEM, table), (VMEM, back), (VMEM, blocks)],
         [(VMEM, (fd, slab + width), f32), (VMEM, (fd, slab), bf16)],
+        [pltpu.VMEM((fd, slab + LANE), f32)] * (BUFFERS - 1),
     )
     got = lax.ppermute(send, "row", SWAP)
-    (own,) = call(
+    own = call(
         keep_kernel,
         "keep",
         [(VMEM, table), (VMEM, blocks), (VMEM, dagg)],
-        [(VMEM, (fd, slab + LANE), f32)],
+        [(VMEM, (fd, slab + LANE), f32)] * BUFFERS,
     )
     scale = 1.0 / (slab * lax.axis_size("row")) ** 0.5
     output, grad_features, grad_weight = call(
         functools.partial(merge_kernel, slots, scale),
         "merge",
-        [(VMEM, back), (VMEM, own), (VMEM, send), (VMEM, got)],
+        [(VMEM, x) for x in (back, send, got, *own)],
         [(VMEM, (fd, slab), bf16), (VMEM, (fd, slab), bf16), (VMEM, (fd, width), f32)],
     )
     return output, grad_weight, grad_features

time: 44.1 us -> 44.1 us (level)
  no operation moved by 1% of the time
where the time goes in v8:
time: 44.1 us; the launch traced here: 43.9 us
  blocking collectives  33.1 us (75%)
  Pallas kernels  5.31 us (12%)
  starting transfers between devices  4.27 us (10%)
  between operations  0.66 us (1%)
  waiting for transfers between devices  0.57 us (1%)
    all_to_all x2, blocking collectives, exchange(): lax.all_to_all(message, 'col', 0, 0, tiled=True, axis_index_groups=[listed])  33.1 us
    pallas_call x6, Pallas kernels, call(): pl.pallas_call(kernel, in_specs=[space for space, _ in operands], out_spe...  5.31 us
    ppermute x1, starting transfers between devices, local(): got = lax.ppermute(send, 'row', SWAP)  2.81 us
    ppermute x1, starting transfers between devices, local(): other = lax.ppermute(features, 'row', SWAP)  1.46 us
  transfers between devices with their start and end apart: 2, of which 1 were waited for; matrix products, arithmetic and copies ran while one was open for 0% of the time, Pallas kernels for 7%

profile of v8, /device:TPU:1, one launch (start us, length us, event | category | flops | bytes accessed | tf_op | source)
XLA Modules:
  0.0 43.9 jit_solution(13857108688650309965)
XLA Ops:
  0.6 1.5 %collective-permute-start = (bf16[8,4096]{1,0:T(8,128)(2,1)}, bf16[8,4096]{1,0:T(8,128)(2,1)S(1)}, u32[]{:S(2)}, u32[]{:S(2)}) collective-permute-start(bf16[8,4096]{1,0:T(8,128)(2,1)} %own_hbm.1), channel_id=1, source_target_pairs={{0,64},{64,0},{1,65},{65,1},{2,66},{66,2},{3,67},{67,3},{4,68},{68... | collective-permute-start | bytes 196616 | tf_op jit(solution)/shard_map/ppermute | solution.py:264
  2.1 2.4 %first.1 = (s32[2,64,128]{2,1,0:T(8,128)S(1)}, bf16[32,2,2,128,128]{4,3,2,1,0:T(8,128)(2,1)S(1)}, f32[8,4096]{1,0:T(8,128)S(1)}, bf16[64,4,896]{2,1,0:T(4,128)(2,1)S(1)}) custom-call(s32[2,2,32]{2,1,0:T(2,128)} %bitcast.2, s32[2,32]{1,0:T(2,128)} %bitcast.3, bf16[8,4096]{1,0:T(8,128)(2,1)} %own_hbm.1, bf16[8,512]{1,0:T(8,128)(2,1)} %weight_hbm.1, ...), custom_call_target="tpu_custom_call" | custom-call | tf_op jit(solution)/shard_map/first/pallas_call | solution.py:243
  4.5 0.0 collective-permute-done.other
  4.6 0.7 %second.1 = bf16[64,4,896]{2,1,0:T(4,128)(2,1)S(1)} custom-call(s32[2,64,128]{2,1,0:T(8,128)S(1)} %get-tuple-element.14.table, bf16[8,4096]{1,0:T(8,128)(2,1)S(1)} %collective-permute-done.other, bf16[32,2,2,128,128]{4,3,2,1,0:T(8,128)(2,1)S(1)} %get-tuple-element.15.a_ref, f32[8,4096]{1,0:T(8,128)S(1)} %get-tuple-element.16.part, ...), custom_call_target="tpu_custom_call", output_to_operand_aliasing={{}: (4, {})} | custom-call | tf_op jit(solution)/shard_map/second/pallas_call | solution.py:243
  5.3 18.3 %all_to_all.10.msg = bf16[64,4,896]{2,1,0:T(4,128)(2,1)S(1)} all-to-all(bf16[64,4,896]{2,1,0:T(4,128)(2,1)S(1)} %second.1), channel_id=1, replica_groups={{58,10,56,63,55,48,4,54,34,0,3,5,27,44,50,33,14,62,30,19,42,60,12,28,24..., dimensions={0} | all-to-all | bytes 917504 | tf_op jit(solution)/shard_map/all_to_all | solution.py:33
  23.6 0.5 %dense.1 = bf16[64,4,896]{2,1,0:T(4,128)(2,1)S(1)} custom-call(bf16[64,4,896]{2,1,0:T(4,128)(2,1)S(1)} %all_to_all.10.msg), custom_call_target="tpu_custom_call" | custom-call | tf_op jit(solution)/shard_map/dense/pallas_call | solution.py:243
  24.1 14.7 %all_to_all.11.back = bf16[64,4,896]{2,1,0:T(4,128)(2,1)S(1)} all-to-all(bf16[64,4,896]{2,1,0:T(4,128)(2,1)S(1)} %dense.1), channel_id=1, replica_groups={{58,10,56,63,55,48,4,54,34,0,3,5,27,44,50,33,14,62,30,19,42,60,12,28,24..., dimensions={0} | all-to-all | bytes 917504 | tf_op jit(solution)/shard_map/all_to_all | solution.py:33
  38.9 0.5 %send.1 = (f32[8,4608]{1,0:T(8,128)S(1)}, bf16[8,4096]{1,0:T(8,128)(2,1)S(1)}) custom-call(s32[2,64,128]{2,1,0:T(8,128)S(1)} %get-tuple-element.14.table, bf16[64,4,896]{2,1,0:T(4,128)(2,1)S(1)} %all_to_all.11.back, bf16[32,2,2,128,128]{4,3,2,1,0:T(8,128)(2,1)S(1)} %get-tuple-element.15.a_ref), custom_call_target="tpu_custom_call" | custom-call | tf_op jit(solution)/shard_map/send/pallas_call | solution.py:243
  39.4 2.8 %collective-permute-start.1 = (f32[8,4608]{1,0:T(8,128)S(1)}, f32[8,4608]{1,0:T(8,128)S(1)}, u32[]{:S(2)}, u32[]{:S(2)}) collective-permute-start(f32[8,4608]{1,0:T(8,128)S(1)} %get-tuple-element.18.sent), channel_id=1, source_target_pairs={{0,64},{64,0},{1,65},{65,1},{2,66},{66,2},{3,67},{67,3},{4,68},{68... | collective-permute-start | bytes 442376 | tf_op jit(solution)/shard_map/ppermute | solution.py:309
  42.2 0.4 keep.1
  42.6 0.6 %collective-permute-done.1.got = f32[8,4608]{1,0:T(8,128)S(1)} collective-permute-done((f32[8,4608]{1,0:T(8,128)S(1)}, f32[8,4608]{1,0:T(8,128)S(1)}, u32[]{:S(2)}, u32[]{:S(2)}) %collective-permute-start.1) | collective-permute-done | bytes 147488 | tf_op jit(solution)/shard_map/ppermute | solution.py:309
  43.2 0.7 %merge.1 = (bf16[8,4096]{1,0:T(8,128)(2,1)}, bf16[8,4096]{1,0:T(8,128)(2,1)}, f32[8,512]{1,0:T(8,128)}) custom-call(bf16[64,4,896]{2,1,0:T(4,128)(2,1)S(1)} %all_to_all.11.back, f32[8,4608]{1,0:T(8,128)S(1)} %get-tuple-element.18.sent, f32[8,4608]{1,0:T(8,128)S(1)} %collective-permute-done.1.got, f32[8,4224]{1,0:T(8,128)S(1)} %get-tuple-element.20.refs_0_, ...), custom_call_target="tpu_custom_call" | custom-call | tf_op jit(solution)/shard_map/merge/pallas_call | solution.py:243
Async XLA Ops:
  0.6 3.9 %collective-permute-start = (bf16[8,4096]{1,0:T(8,128)(2,1)}, bf16[8,4096]{1,0:T(8,128)(2,1)S(1)}, u32[]{:S(2)}, u32[]{:S(2)}) collective-permute-start(bf16[8,4096]{1,0:T(8,128)(2,1)} %own_hbm.1), channel_id=1, source_target_pairs={{0,64},{64,0},{1,65},{65,1},{2,66},{66,2},{3,67},{67,3},{4,68},{68... | collective-permute-start | bytes 196616 | tf_op jit(solution)/shard_map/ppermute | solution.py:264
  39.4 3.8 %collective-permute-start.1 = (f32[8,4608]{1,0:T(8,128)S(1)}, f32[8,4608]{1,0:T(8,128)S(1)}, u32[]{:S(2)}, u32[]{:S(2)}) collective-permute-start(f32[8,4608]{1,0:T(8,128)S(1)} %get-tuple-element.18.sent), channel_id=1, source_target_pairs={{0,64},{64,0},{1,65},{65,1},{2,66},{66,2},{3,67},{67,3},{4,68},{68... | collective-permute-start | bytes 442376 | tf_op jit(solution)/shard_map/ppermute | solution.py:309

commit v9 on v8

--- a/solution.py
+++ b/solution.py
@@ -212,22 +212,26 @@
     send[:, slab:] = jnp.concatenate(grads, 0)
 
 
-def keep_kernel(table, a_ref, dagg_ref, *own):
+def keep_kernel(slots, table, back, a_ref, dagg_ref, out_hbm, *refs):
+    own, (out, sem) = refs[:-2], refs[-2:]
     row = lax.axis_index("row")
+    for b in range(len(slots) // 2):
+        tiles = [
+            back[slots[2 * b + q], :, 2 * LANE : 3 * LANE].astype(jnp.float32) for q in range(2)
+        ]
+        out[:, b * LANE : (b + 1) * LANE] = jnp.concatenate(tiles, 0).astype(jnp.bfloat16)
+    copy = pltpu.make_async_copy(out, out_hbm, sem)
+    copy.start()
     blocks = a_ref.shape[0]
     for buffer in own:
         buffer[...] = jnp.zeros_like(buffer)
     for b in range(blocks):
         spread(table, dagg_ref[:, b * LANE : (b + 1) * LANE], a_ref, row, b, own)
-
-
-def merge_kernel(slots, scale, back, sent, got, *refs):
-    own, (out, grad_features, grad_weight) = refs[:-3], refs[-3:]
-    for b in range(len(slots) // 2):
-        tiles = [
-            back[slots[2 * b + q], :, 2 * LANE : 3 * LANE].astype(jnp.float32) for q in range(2)
-        ]
-        out[:, b * LANE : (b + 1) * LANE] = jnp.concatenate(tiles, 0).astype(jnp.bfloat16)
+    copy.wait()
+
+
+def merge_kernel(scale, sent, got, *refs):
+    own, (grad_features, grad_weight) = refs[:-2], refs[-2:]
     slab = grad_features.shape[1]
     total = got[:, :slab]
     for buffer in own:
@@ -307,18 +311,19 @@
         [pltpu.VMEM((fd, slab + LANE), f32)] * (BUFFERS - 1),
     )
     got = lax.ppermute(send, "row", SWAP)
-    own = call(
-        keep_kernel,
+    output, *own = call(
+        functools.partial(keep_kernel, slots),
         "keep",
-        [(VMEM, table), (VMEM, blocks), (VMEM, dagg)],
-        [(VMEM, (fd, slab + LANE), f32)] * BUFFERS,
+        [(VMEM, x) for x in (table, back, blocks, dagg)],
+        [(HBM, (fd, slab), bf16)] + [(VMEM, (fd, slab + LANE), f32)] * BUFFERS,
+        [pltpu.VMEM((fd, slab), bf16), pltpu.SemaphoreType.DMA],
     )
     scale = 1.0 / (slab * lax.axis_size("row")) ** 0.5
-    output, grad_features, grad_weight = call(
-        functools.partial(merge_kernel, slots, scale),
+    grad_features, grad_weight = call(
+        functools.partial(merge_kernel, scale),
         "merge",
-        [(VMEM, x) for x in (back, send, got, *own)],
-        [(VMEM, (fd, slab), bf16), (VMEM, (fd, slab), bf16), (VMEM, (fd, width), f32)],
+        [(VMEM, x) for x in (send, got, *own)],
+        [(VMEM, (fd, slab), bf16), (VMEM, (fd, width), f32)],
     )
     return output, grad_weight, grad_features
 

time: 44.1 us -> 44.1 us (level)
  Pallas kernels: 5.31 us -> 5.89 us
  waiting for transfers between devices: 0.57 us -> 0.01 us
    pallas_call x6, Pallas kernels: 5.31 us -> 5.89 us  [call(): pl.pallas_call(kernel, in_specs=[space for space, _ in operands], out_spe...]
    ppermute x1, waiting for transfers between devices: 0.57 us -> 0.01 us  [local(): got = lax.ppermute(send, 'row', SWAP)]
  transfers between devices with their start and end apart: 2 -> 2, of which waited for: 1 -> 0; matrix products, arithmetic and copies ran while one was open for 0% -> 0% of each run, Pallas kernels for 7% -> 8%
where the time goes in v9:
time: 44.1 us; the launch traced here: 43.9 us
  blocking collectives  33.1 us (75%)
  Pallas kernels  5.89 us (13%)
  starting transfers between devices  4.27 us (10%)
  between operations  0.67 us (2%)
    all_to_all x2, blocking collectives, exchange(): lax.all_to_all(message, 'col', 0, 0, tiled=True, axis_index_groups=[listed])  33.1 us
    pallas_call x6, Pallas kernels, call(): pl.pallas_call(kernel, in_specs=[space for space, _ in operands], out_spe...  5.89 us
    ppermute x1, starting transfers between devices, local(): got = lax.ppermute(send, 'row', SWAP)  2.8 us
    ppermute x1, starting transfers between devices, local(): other = lax.ppermute(features, 'row', SWAP)  1.46 us
  transfers between devices with their start and end apart: 2, of which 0 were waited for; matrix products, arithmetic and copies ran while one was open for 0% of the time, Pallas kernels for 8%

profile of v9, /device:TPU:1, one launch (start us, length us, event | category | flops | bytes accessed | tf_op | source)
XLA Modules:
  0.0 43.9 jit_solution(11338657661874587495)
XLA Ops:
  0.6 1.5 %collective-permute-start = (bf16[8,4096]{1,0:T(8,128)(2,1)}, bf16[8,4096]{1,0:T(8,128)(2,1)S(1)}, u32[]{:S(2)}, u32[]{:S(2)}) collective-permute-start(bf16[8,4096]{1,0:T(8,128)(2,1)} %own_hbm.1), channel_id=1, source_target_pairs={{0,64},{64,0},{1,65},{65,1},{2,66},{66,2},{3,67},{67,3},{4,68},{68... | collective-permute-start | bytes 196616 | tf_op jit(solution)/shard_map/ppermute | solution.py:268
  2.1 2.5 %first.1 = (s32[2,64,128]{2,1,0:T(8,128)S(1)}, bf16[32,2,2,128,128]{4,3,2,1,0:T(8,128)(2,1)S(1)}, f32[8,4096]{1,0:T(8,128)S(1)}, bf16[64,4,896]{2,1,0:T(4,128)(2,1)S(1)}) custom-call(s32[2,2,32]{2,1,0:T(2,128)} %bitcast.2, s32[2,32]{1,0:T(2,128)} %bitcast.3, bf16[8,4096]{1,0:T(8,128)(2,1)} %own_hbm.1, bf16[8,512]{1,0:T(8,128)(2,1)} %weight_hbm.1, ...), custom_call_target="tpu_custom_call" | custom-call | tf_op jit(solution)/shard_map/first/pallas_call | solution.py:247
  4.6 0.0 collective-permute-done.other
  4.6 0.7 %second.1 = bf16[64,4,896]{2,1,0:T(4,128)(2,1)S(1)} custom-call(s32[2,64,128]{2,1,0:T(8,128)S(1)} %get-tuple-element.14.table, bf16[8,4096]{1,0:T(8,128)(2,1)S(1)} %collective-permute-done.other, bf16[32,2,2,128,128]{4,3,2,1,0:T(8,128)(2,1)S(1)} %get-tuple-element.15.a_ref, f32[8,4096]{1,0:T(8,128)S(1)} %get-tuple-element.16.part, ...), custom_call_target="tpu_custom_call", output_to_operand_aliasing={{}: (4, {})} | custom-call | tf_op jit(solution)/shard_map/second/pallas_call | solution.py:247
  5.3 18.3 %all_to_all.10.msg = bf16[64,4,896]{2,1,0:T(4,128)(2,1)S(1)} all-to-all(bf16[64,4,896]{2,1,0:T(4,128)(2,1)S(1)} %second.1), channel_id=1, replica_groups={{58,10,56,63,55,48,4,54,34,0,3,5,27,44,50,33,14,62,30,19,42,60,12,28,24..., dimensions={0} | all-to-all | bytes 917504 | tf_op jit(solution)/shard_map/all_to_all | solution.py:33
  23.6 0.5 %dense.1 = bf16[64,4,896]{2,1,0:T(4,128)(2,1)S(1)} custom-call(bf16[64,4,896]{2,1,0:T(4,128)(2,1)S(1)} %all_to_all.10.msg), custom_call_target="tpu_custom_call" | custom-call | tf_op jit(solution)/shard_map/dense/pallas_call | solution.py:247
  24.2 14.8 %all_to_all.11.back = bf16[64,4,896]{2,1,0:T(4,128)(2,1)S(1)} all-to-all(bf16[64,4,896]{2,1,0:T(4,128)(2,1)S(1)} %dense.1), channel_id=1, replica_groups={{58,10,56,63,55,48,4,54,34,0,3,5,27,44,50,33,14,62,30,19,42,60,12,28,24..., dimensions={0} | all-to-all | bytes 917504 | tf_op jit(solution)/shard_map/all_to_all | solution.py:33
  38.9 0.5 %send.1 = (f32[8,4608]{1,0:T(8,128)S(1)}, bf16[8,4096]{1,0:T(8,128)(2,1)S(1)}) custom-call(s32[2,64,128]{2,1,0:T(8,128)S(1)} %get-tuple-element.14.table, bf16[64,4,896]{2,1,0:T(4,128)(2,1)S(1)} %all_to_all.11.back, bf16[32,2,2,128,128]{4,3,2,1,0:T(8,128)(2,1)S(1)} %get-tuple-element.15.a_ref), custom_call_target="tpu_custom_call" | custom-call | tf_op jit(solution)/shard_map/send/pallas_call | solution.py:247
  39.4 2.8 %collective-permute-start.1 = (f32[8,4608]{1,0:T(8,128)S(1)}, f32[8,4608]{1,0:T(8,128)S(1)}, u32[]{:S(2)}, u32[]{:S(2)}) collective-permute-start(f32[8,4608]{1,0:T(8,128)S(1)} %get-tuple-element.20.sent), channel_id=1, source_target_pairs={{0,64},{64,0},{1,65},{65,1},{2,66},{66,2},{3,67},{67,3},{4,68},{68... | collective-permute-start | bytes 442376 | tf_op jit(solution)/shard_map/ppermute | solution.py:313
  42.2 1.0 %keep.1 = (bf16[8,4096]{1,0:T(8,128)(2,1)}, f32[8,4224]{1,0:T(8,128)S(1)}, f32[8,4224]{1,0:T(8,128)S(1)}) custom-call(s32[2,64,128]{2,1,0:T(8,128)S(1)} %get-tuple-element.14.table, bf16[64,4,896]{2,1,0:T(4,128)(2,1)S(1)} %all_to_all.11.back, bf16[32,2,2,128,128]{4,3,2,1,0:T(8,128)(2,1)S(1)} %get-tuple-element.15.a_ref, ...), custom_call_target="tpu_custom_call" | custom-call | tf_op jit(solution)/shard_map/keep/pallas_call | solution.py:247
  43.2 0.0 collective-permute-done.1.got
  43.2 0.7 %merge.1 = (bf16[8,4096]{1,0:T(8,128)(2,1)}, f32[8,512]{1,0:T(8,128)}) custom-call(f32[8,4608]{1,0:T(8,128)S(1)} %get-tuple-element.20.sent, f32[8,4608]{1,0:T(8,128)S(1)} %collective-permute-done.1.got, f32[8,4224]{1,0:T(8,128)S(1)} %get-tuple-element.21.refs_0_, f32[8,4224]{1,0:T(8,128)S(1)} %get-tuple-element.22.refs_1_), custom_call_target="tpu_custom_call" | custom-call | tf_op jit(solution)/shard_map/merge/pallas_call | solution.py:247
Async XLA Ops:
  0.6 3.9 %collective-permute-start = (bf16[8,4096]{1,0:T(8,128)(2,1)}, bf16[8,4096]{1,0:T(8,128)(2,1)S(1)}, u32[]{:S(2)}, u32[]{:S(2)}) collective-permute-start(bf16[8,4096]{1,0:T(8,128)(2,1)} %own_hbm.1), channel_id=1, source_target_pairs={{0,64},{64,0},{1,65},{65,1},{2,66},{66,2},{3,67},{67,3},{4,68},{68... | collective-permute-start | bytes 196616 | tf_op jit(solution)/shard_map/ppermute | solution.py:268
  39.4 3.8 %collective-permute-start.1 = (f32[8,4608]{1,0:T(8,128)S(1)}, f32[8,4608]{1,0:T(8,128)S(1)}, u32[]{:S(2)}, u32[]{:S(2)}) collective-permute-start(f32[8,4608]{1,0:T(8,128)S(1)} %get-tuple-element.20.sent), channel_id=1, source_target_pairs={{0,64},{64,0},{1,65},{65,1},{2,66},{66,2},{3,67},{67,3},{4,68},{68... | collective-permute-start | bytes 442376 | tf_op jit(solution)/shard_map/ppermute | solution.py:313

commit v10 on v9

--- a/solution.py
+++ b/solution.py
@@ -13,10 +13,10 @@
 LANE = 128
 BUFFERS = 2
 ORDER_SEED = (
-    58, 10, 56, 63, 55, 48, 4, 54, 34, 0, 3, 5, 27, 44, 50, 33,
-    14, 62, 30, 19, 42, 60, 12, 28, 24, 37, 61, 36, 47, 35, 45, 7,
-    8, 6, 41, 22, 51, 57, 46, 15, 39, 16, 52, 59, 49, 1, 13, 38,
-    31, 53, 2, 11, 20, 40, 29, 9, 17, 26, 21, 25, 23, 32, 18, 43,
+    58, 6, 0, 38, 4, 25, 16, 49, 13, 43, 10, 51, 34, 32, 56, 31,
+    18, 37, 17, 30, 52, 45, 23, 33, 55, 5, 47, 26, 29, 35, 53, 54,
+    7, 44, 27, 50, 2, 1, 41, 8, 19, 24, 12, 46, 22, 9, 21, 40,
+    14, 39, 3, 28, 62, 59, 61, 57, 60, 48, 42, 36, 20, 63, 15, 11,
 )
 
 

time: 44.1 us -> 44.1 us (level)
  no operation moved by 1% of the time
where the time goes in v10:
time: 44.1 us; the launch traced here: 43.9 us
  blocking collectives  33.4 us (76%)
  Pallas kernels  5.88 us (13%)
  starting transfers between devices  3.96 us (9%)
  between operations  0.67 us (2%)
    all_to_all x2, blocking collectives, exchange(): lax.all_to_all(message, 'col', 0, 0, tiled=True, axis_index_groups=[listed])  33.4 us
    pallas_call x6, Pallas kernels, call(): pl.pallas_call(kernel, in_specs=[space for space, _ in operands], out_spe...  5.88 us
    ppermute x1, starting transfers between devices, local(): got = lax.ppermute(send, 'row', SWAP)  2.5 us
    ppermute x1, starting transfers between devices, local(): other = lax.ppermute(features, 'row', SWAP)  1.46 us
  transfers between devices with their start and end apart: 2, of which 0 were waited for; matrix products, arithmetic and copies ran while one was open for 0% of the time, Pallas kernels for 8%

profile of v10, /device:TPU:1, one launch (start us, length us, event | category | flops | bytes accessed | tf_op | source)
XLA Modules:
  0.0 43.9 jit_solution(14761032260384505252)
XLA Ops:
  0.6 1.5 %collective-permute-start = (bf16[8,4096]{1,0:T(8,128)(2,1)}, bf16[8,4096]{1,0:T(8,128)(2,1)S(1)}, u32[]{:S(2)}, u32[]{:S(2)}) collective-permute-start(bf16[8,4096]{1,0:T(8,128)(2,1)} %own_hbm.1), channel_id=1, source_target_pairs={{0,64},{64,0},{1,65},{65,1},{2,66},{66,2},{3,67},{67,3},{4,68},{68... | collective-permute-start | bytes 196616 | tf_op jit(solution)/shard_map/ppermute | solution.py:268
  2.1 2.5 %first.1 = (s32[2,64,128]{2,1,0:T(8,128)S(1)}, bf16[32,2,2,128,128]{4,3,2,1,0:T(8,128)(2,1)S(1)}, f32[8,4096]{1,0:T(8,128)S(1)}, bf16[64,4,896]{2,1,0:T(4,128)(2,1)S(1)}) custom-call(s32[2,2,32]{2,1,0:T(2,128)} %bitcast.2, s32[2,32]{1,0:T(2,128)} %bitcast.3, bf16[8,4096]{1,0:T(8,128)(2,1)} %own_hbm.1, bf16[8,512]{1,0:T(8,128)(2,1)} %weight_hbm.1, ...), custom_call_target="tpu_custom_call" | custom-call | tf_op jit(solution)/shard_map/first/pallas_call | solution.py:247
  4.6 0.0 collective-permute-done.other
  4.6 0.7 %second.1 = bf16[64,4,896]{2,1,0:T(4,128)(2,1)S(1)} custom-call(s32[2,64,128]{2,1,0:T(8,128)S(1)} %get-tuple-element.14.table, bf16[8,4096]{1,0:T(8,128)(2,1)S(1)} %collective-permute-done.other, bf16[32,2,2,128,128]{4,3,2,1,0:T(8,128)(2,1)S(1)} %get-tuple-element.15.a_ref, f32[8,4096]{1,0:T(8,128)S(1)} %get-tuple-element.16.part, ...), custom_call_target="tpu_custom_call", output_to_operand_aliasing={{}: (4, {})} | custom-call | tf_op jit(solution)/shard_map/second/pallas_call | solution.py:247
  5.3 18.3 %all_to_all.10.msg = bf16[64,4,896]{2,1,0:T(4,128)(2,1)S(1)} all-to-all(bf16[64,4,896]{2,1,0:T(4,128)(2,1)S(1)} %second.1), channel_id=1, replica_groups={{58,6,0,38,4,25,16,49,13,43,10,51,34,32,56,31,18,37,17,30,52,45,23,33,5..., dimensions={0} | all-to-all | bytes 917504 | tf_op jit(solution)/shard_map/all_to_all | solution.py:33
  23.6 0.5 %dense.1 = bf16[64,4,896]{2,1,0:T(4,128)(2,1)S(1)} custom-call(bf16[64,4,896]{2,1,0:T(4,128)(2,1)S(1)} %all_to_all.10.msg), custom_call_target="tpu_custom_call" | custom-call | tf_op jit(solution)/shard_map/dense/pallas_call | solution.py:247
  24.2 15.0 %all_to_all.11.back = bf16[64,4,896]{2,1,0:T(4,128)(2,1)S(1)} all-to-all(bf16[64,4,896]{2,1,0:T(4,128)(2,1)S(1)} %dense.1), channel_id=1, replica_groups={{58,6,0,38,4,25,16,49,13,43,10,51,34,32,56,31,18,37,17,30,52,45,23,33,5..., dimensions={0} | all-to-all | bytes 917504 | tf_op jit(solution)/shard_map/all_to_all | solution.py:33
  39.2 0.5 %send.1 = (f32[8,4608]{1,0:T(8,128)S(1)}, bf16[8,4096]{1,0:T(8,128)(2,1)S(1)}) custom-call(s32[2,64,128]{2,1,0:T(8,128)S(1)} %get-tuple-element.14.table, bf16[64,4,896]{2,1,0:T(4,128)(2,1)S(1)} %all_to_all.11.back, bf16[32,2,2,128,128]{4,3,2,1,0:T(8,128)(2,1)S(1)} %get-tuple-element.15.a_ref), custom_call_target="tpu_custom_call" | custom-call | tf_op jit(solution)/shard_map/send/pallas_call | solution.py:247
  39.7 2.5 %collective-permute-start.1 = (f32[8,4608]{1,0:T(8,128)S(1)}, f32[8,4608]{1,0:T(8,128)S(1)}, u32[]{:S(2)}, u32[]{:S(2)}) collective-permute-start(f32[8,4608]{1,0:T(8,128)S(1)} %get-tuple-element.20.sent), channel_id=1, source_target_pairs={{0,64},{64,0},{1,65},{65,1},{2,66},{66,2},{3,67},{67,3},{4,68},{68... | collective-permute-start | bytes 442376 | tf_op jit(solution)/shard_map/ppermute | solution.py:313
  42.2 1.0 %keep.1 = (bf16[8,4096]{1,0:T(8,128)(2,1)}, f32[8,4224]{1,0:T(8,128)S(1)}, f32[8,4224]{1,0:T(8,128)S(1)}) custom-call(s32[2,64,128]{2,1,0:T(8,128)S(1)} %get-tuple-element.14.table, bf16[64,4,896]{2,1,0:T(4,128)(2,1)S(1)} %all_to_all.11.back, bf16[32,2,2,128,128]{4,3,2,1,0:T(8,128)(2,1)S(1)} %get-tuple-element.15.a_ref, ...), custom_call_target="tpu_custom_call" | custom-call | tf_op jit(solution)/shard_map/keep/pallas_call | solution.py:247
  43.2 0.0 collective-permute-done.1.got
  43.2 0.7 %merge.1 = (bf16[8,4096]{1,0:T(8,128)(2,1)}, f32[8,512]{1,0:T(8,128)}) custom-call(f32[8,4608]{1,0:T(8,128)S(1)} %get-tuple-element.20.sent, f32[8,4608]{1,0:T(8,128)S(1)} %collective-permute-done.1.got, f32[8,4224]{1,0:T(8,128)S(1)} %get-tuple-element.21.refs_0_, f32[8,4224]{1,0:T(8,128)S(1)} %get-tuple-element.22.refs_1_), custom_call_target="tpu_custom_call" | custom-call | tf_op jit(solution)/shard_map/merge/pallas_call | solution.py:247
Async XLA Ops:
  0.6 3.9 %collective-permute-start = (bf16[8,4096]{1,0:T(8,128)(2,1)}, bf16[8,4096]{1,0:T(8,128)(2,1)S(1)}, u32[]{:S(2)}, u32[]{:S(2)}) collective-permute-start(bf16[8,4096]{1,0:T(8,128)(2,1)} %own_hbm.1), channel_id=1, source_target_pairs={{0,64},{64,0},{1,65},{65,1},{2,66},{66,2},{3,67},{67,3},{4,68},{68... | collective-permute-start | bytes 196616 | tf_op jit(solution)/shard_map/ppermute | solution.py:268
  39.7 3.5 %collective-permute-start.1 = (f32[8,4608]{1,0:T(8,128)S(1)}, f32[8,4608]{1,0:T(8,128)S(1)}, u32[]{:S(2)}, u32[]{:S(2)}) collective-permute-start(f32[8,4608]{1,0:T(8,128)S(1)} %get-tuple-element.20.sent), channel_id=1, source_target_pairs={{0,64},{64,0},{1,65},{65,1},{2,66},{66,2},{3,67},{67,3},{4,68},{68... | collective-permute-start | bytes 442376 | tf_op jit(solution)/shard_map/ppermute | solution.py:313
